TPU v7x, 256 devices: a whole 4x4x8 slice. The times are simulated.
256 devices in a mesh: seq: 32 (over x, z), hid: 8 (over y, core).
Axes of the slice: x: 4, y: 4, z: 8, core: 2. Of those that a mesh axis runs over, the one named last changes fastest.
Arguments:
- tokens: bfloat16 [4096, 4096], P('seq', 'hid'), may hold values from -6 to 6
- hidden_grad: bfloat16 [4096, 14336], P('seq', 'hid'), may hold values from -6 to 6
- gate_blocks: bfloat16 [8, 224, 128, 128], P('hid', 'seq'), may hold values from -0.125 to 0.125
- up_blocks: bfloat16 [8, 224, 128, 128], P('hid', 'seq'), may hold values from -0.125 to 0.125
- gate_rows: int32 [8, 224], P('hid'), may hold values from 0 to 31, as said below
- gate_cols: int32 [8, 224], P('hid'), may hold values from 0 to 13
- gate_count: int32 [8], P('hid'), may hold values from 28 to 224, as said below
- up_rows: int32 [8, 224], P('hid'), may hold values from 0 to 31, as said below
- up_cols: int32 [8, 224], P('hid'), may hold values from 0 to 13
- up_count: int32 [8], P('hid'), may hold values from 28 to 224, as said below
Outputs:
- hidden: bfloat16 [4096, 14336], P('seq', 'hid')
- input_grad: bfloat16 [4096, 4096], P('seq', 'hid')
- gate_block_grads: bfloat16 [8, 224, 128, 128], P('hid', 'seq')
- up_block_grads: bfloat16 [8, 224, 128, 128], P('hid', 'seq')
Inputs may be any that keep to these rules, and one draw needn't show every extreme that they name: For each panel, the pairs (gate_rows, gate_cols) over all 224 slots are distinct. `gate_count`: slots at or after a panel's count hold no block of the matrix. For each panel, the pairs (up_rows, up_cols) over all 224 slots are distinct. `up_count`: slots at or after a panel's count hold no block of the matrix.
All inputs are finite; a program needn't handle non-finite values.
Results may differ from a plain program's by a relative error of at most 0.018.
Values may be sent and summed in bfloat16 or wider, within the bound.
No kernel may reach another device: no remote copies, remote signals or barrier semaphores. Data moves between devices by JAX's collectives and lax.ppermute only.
A program may use at most 128 MiB of HBM per device.

v0:
```python
import math

import jax
import jax.numpy as jnp
from jax import lax
from jax.sharding import PartitionSpec as P


def silu_parts(preact):
    sigma = jax.nn.sigmoid(preact)
    return (preact * sigma, sigma * (1.0 + preact * (1.0 - sigma)))


def place_split(products, placing, form):
    high_part = products.astype(jnp.bfloat16)
    rest_part = (products - high_part.astype(jnp.float32)).astype(jnp.bfloat16)
    table = placing.astype(jnp.bfloat16)
    placed = jnp.einsum(form, high_part, table, preferred_element_type=jnp.float32)
    return placed + jnp.einsum(form, rest_part, table, preferred_element_type=jnp.float32)


def project_slots(tiles, weights, rows, columns, live_count, group_size, trips, col_blocks):
    tok_rows = tiles.shape[0]
    block_size = tiles.shape[2]
    targets = jnp.arange(col_blocks)
    offsets = jnp.arange(group_size)

    def project_one_group(group_index, running):
        start = group_index * group_size
        chosen = lax.dynamic_slice_in_dim(weights, start, group_size, 0)
        row_ids = lax.dynamic_slice_in_dim(rows, start, group_size, 0)
        col_ids = lax.dynamic_slice_in_dim(columns, start, group_size, 0)
        active = start + offsets < live_count
        picked = jnp.take(tiles, row_ids, axis=1)
        products = jnp.einsum("tsk,skn->tsn", picked, chosen, preferred_element_type=jnp.float32)
        placing = (col_ids[:, None] == targets[None, :]) & active[:, None]
        return running + place_split(products, placing, "tsn,sc->tcn")

    initial = jnp.zeros((tok_rows, col_blocks, block_size), jnp.float32)
    return lax.fori_loop(0, trips, project_one_group, initial)


def return_slots(grad_tiles, weights, rows, columns, live_count, group_size, trips, row_blocks):
    tok_rows = grad_tiles.shape[0]
    block_size = grad_tiles.shape[2]
    targets = jnp.arange(row_blocks)
    offsets = jnp.arange(group_size)

    def return_one_group(group_index, running):
        start = group_index * group_size
        chosen = lax.dynamic_slice_in_dim(weights, start, group_size, 0)
        row_ids = lax.dynamic_slice_in_dim(rows, start, group_size, 0)
        col_ids = lax.dynamic_slice_in_dim(columns, start, group_size, 0)
        active = start + offsets < live_count
        picked = jnp.take(grad_tiles, col_ids, axis=1)
        products = jnp.einsum("tsn,skn->tsk", picked, chosen, preferred_element_type=jnp.float32)
        placing = (row_ids[:, None] == targets[None, :]) & active[:, None]
        return running + place_split(products, placing, "tsk,sr->trk")

    initial = jnp.zeros((tok_rows, row_blocks, block_size), jnp.float32)
    return lax.fori_loop(0, trips, return_one_group, initial)


def on_device(
    tokens,
    hidden_grad,
    gate_blocks,
    up_blocks,
    gate_rows,
    gate_cols,
    gate_count,
    up_rows,
    up_cols,
    up_count,
):
    gathered = lax.all_gather(tokens, "hid", axis=1, tiled=True)
    tok_rows = gathered.shape[0]
    block_size = gate_blocks.shape[2]
    row_blocks = gathered.shape[1] // block_size
    col_blocks = hidden_grad.shape[1] // block_size
    gate_all = lax.all_gather(gate_blocks, "seq", axis=1, tiled=True)
    up_all = lax.all_gather(up_blocks, "seq", axis=1, tiled=True)
    capacity = gate_all.shape[1]
    group_size = 32
    groups = capacity // group_size
    gate_live = gate_count[0]
    up_live = up_count[0]
    tiles = gathered.reshape(tok_rows, row_blocks, block_size)
    gate_pre = project_slots(
        tiles, gate_all[0], gate_rows[0], gate_cols[0], gate_live, group_size, groups, col_blocks
    )
    up_pre = project_slots(
        tiles, up_all[0], up_rows[0], up_cols[0], up_live, group_size, groups, col_blocks
    )
    activated, slope = silu_parts(gate_pre)
    hidden = (activated * up_pre).astype(jnp.bfloat16)
    upstream = hidden_grad.reshape(tok_rows, col_blocks, block_size).astype(jnp.float32)
    gate_grad = (upstream * up_pre * slope).astype(jnp.bfloat16)
    up_grad = (upstream * activated).astype(jnp.bfloat16)
    input_sum = return_slots(
        gate_grad,
        gate_all[0],
        gate_rows[0],
        gate_cols[0],
        gate_live,
        group_size,
        groups,
        row_blocks,
    )
    input_sum = input_sum + return_slots(
        up_grad, up_all[0], up_rows[0], up_cols[0], up_live, group_size, groups, row_blocks
    )
    input_grad = lax.psum_scatter(
        input_sum.reshape(tok_rows, row_blocks * block_size).astype(jnp.bfloat16),
        "hid",
        scatter_dimension=1,
        tiled=True,
    )
    seq_count = lax.axis_size("seq")
    all_slots = jnp.arange(capacity)
    stacked = []
    for rows, columns, live_count, grad_tiles in (
        (gate_rows[0], gate_cols[0], gate_live, gate_grad),
        (up_rows[0], up_cols[0], up_live, up_grad),
    ):
        row_ids = jnp.take(rows, all_slots)
        col_ids = jnp.take(columns, all_slots)
        picked_input = jnp.take(tiles, row_ids, axis=1)
        picked_grad = jnp.take(grad_tiles, col_ids, axis=1)
        block_term = jnp.einsum(
            "tsk,tsn->skn", picked_input, picked_grad, preferred_element_type=jnp.float32
        )
        stacked.append(block_term * (all_slots < live_count).astype(jnp.float32)[:, None, None])
    partial_value = jnp.stack(stacked, axis=1).astype(jnp.bfloat16)
    shaped = partial_value.reshape((seq_count, capacity // seq_count) + partial_value.shape[1:])
    received = lax.all_to_all(shaped, "seq", split_axis=0, concat_axis=0, tiled=True)
    summed = jnp.sum(received, axis=0, dtype=jnp.float32)
    scale = 1.0 / math.sqrt(tok_rows * seq_count)
    gate_block_grads = (summed[:, 0] * scale).astype(jnp.bfloat16)[None]
    up_block_grads = (summed[:, 1] * scale).astype(jnp.bfloat16)[None]
    return (
        hidden.reshape(tok_rows, col_blocks * block_size),
        input_grad,
        gate_block_grads,
        up_block_grads,
    )


def solution(mesh):
    placed = (
        P("seq", "hid"),
        P("seq", "hid"),
        P("hid", "seq", None, None),
        P("hid", "seq", None, None),
        P("hid", None),
        P("hid", None),
        P("hid"),
        P("hid", None),
        P("hid", None),
        P("hid"),
    )
    return jax.shard_map(
        on_device,
        mesh=mesh,
        in_specs=placed,
        out_specs=(
            P("seq", "hid"),
            P("seq", "hid"),
            P("hid", "seq", None, None),
            P("hid", "seq", None, None),
        ),
        check_vma=False,
    )
```

profile of v0, /device:TPU:179, one launch (start us, length us, event | category | flops | bytes accessed | tf_op | source)
XLA Modules:
  0.0 732.7 jit_solution(12208469907017653431)
XLA Ops:
  22.2 14.1 %all-gather.6.cloned.1.call-done = bf16[128,4096]{0,1:T(8,128)(2,1)} async-done(((bf16[128,512]{0,1:T(8,128)(2,1)}), bf16[128,4096]{0,1:T(8,128)(2,1)}) %all-gather.6.cloned.1.call-update) | async-done | bytes 1048592 | tf_op jit(solution)/shard_map/all_gather | solution.py:76
  38.4 8.4 %gather_fusion.9 = bf16[224,128,128]{2,1,0:T(8,128)(2,1)} fusion(bf16[128,32,128]{2,0,1:T(8,128)(2,1)S(1)} %copy.92, s32[1024]{0:T(1024)S(1)} %pad_clamp_fusion.5), kind=kCustom, calls=%fused_computation.10.clone | custom fusion | bytes 14680960 | tf_op jit(solution)/shard_map/jit(_take)/gather | solution.py:128
  46.8 8.3 %gather_fusion.5 = bf16[224,128,128]{2,1,0:T(8,128)(2,1)} fusion(bf16[128,32,128]{2,0,1:T(8,128)(2,1)S(1)} %copy.92, s32[1024]{0:T(1024)S(1)} %pad_clamp_fusion.7), kind=kCustom, calls=%fused_computation.3.clone | custom fusion | bytes 14680960 | tf_op jit(solution)/shard_map/jit(_take)/gather | solution.py:128
  55.1 74.4 %all-gather.8.cloned.1.call-done = bf16[1,224,128,128]{3,2,0,1:T(8,128)(2,1)} async-done(((bf16[1,7,128,128]{3,2,0,1:T(8,128)(2,1)}), bf16[1,224,128,128]{3,2,0,1:T(8,128)(2,1)}) %all-gather.8.cloned.1.call-update) | async-done | bytes 7340048 | tf_op jit(solution)/shard_map/all_gather | solution.py:82
  129.5 82.0 %while.61 = (s32[]{:T(128)}, f32[128,14,128]{2,1,0:T(8,128)}, s32[224]{0:T(256)S(1)}, s32[]{:T(128)}, bf16[224,128,128]{2,1,0:T(8,128)(2,1)}, /*index=5*/s32[224...) while((s32[]{:T(128)}, f32[128,14,128]{2,1,0:T(8,128)}, ...), condition=%wide.region_3.5_spmd.clone, body=%wide.region_2.4_spmd.clone.sunk | while | flops 166890496 | bytes 16258401 | solution.py:40
  131.1 3.1 fusion.158
  142.5 3.1 fusion.158
  154.2 3.2 fusion.158
  166.0 3.1 fusion.158
  177.7 3.1 fusion.158
  189.5 3.1 fusion.158
  201.2 3.2 fusion.158
  208.7 2.9 fusion.160
  211.5 11.0 %all-gather.4.cloned.1.call-done = bf16[1,224,128,128]{3,2,0,1:T(8,128)(2,1)} async-done(((bf16[1,7,128,128]{3,2,0,1:T(8,128)(2,1)}), bf16[1,224,128,128]{3,2,0,1:T(8,128)(2,1)}) %all-gather.4.cloned.1.call-update) | async-done | bytes 7340048 | tf_op jit(solution)/shard_map/all_gather | solution.py:81
  222.5 82.0 %while.60 = (s32[]{:T(128)}, f32[128,14,128]{2,1,0:T(8,128)}, s32[224]{0:T(256)S(1)}, s32[]{:T(128)}, bf16[224,128,128]{2,1,0:T(8,128)(2,1)}, /*index=5*/s32[224...) while((s32[]{:T(128)}, f32[128,14,128]{2,1,0:T(8,128)}, ...), condition=%wide.region_1.3_spmd.clone, body=%wide.region_0.2_spmd.clone.sunk | while | flops 166890496 | bytes 16258401 | solution.py:40
  224.0 3.1 fusion.151
  235.5 3.1 fusion.151
  242.9 2.8 fusion.153
  247.2 3.1 fusion.151
  259.0 3.1 fusion.151
  266.4 2.8 fusion.153
  270.7 3.1 fusion.151
  278.2 2.8 fusion.153
  282.5 3.1 fusion.151
  289.9 2.8 fusion.153
  294.2 3.1 fusion.151
  307.1 8.5 %gather_fusion.11 = bf16[224,128,128]{2,1,0:T(8,128)(2,1)} fusion(bf16[128,14,128]{2,0,1:T(8,128)(2,1)S(1)} %get-tuple-element.1279, s32[1024]{0:T(1024)S(1)} %pad_clamp_fusion.4), kind=kCustom, calls=%fused_computation.11.clone | custom fusion | bytes 14680960 | tf_op jit(solution)/shard_map/jit(_take)/gather | solution.py:129
  315.6 8.3 %gather_fusion.7 = bf16[224,128,128]{2,1,0:T(8,128)(2,1)} fusion(bf16[128,14,128]{2,0,1:T(8,128)(2,1)S(1)} %get-tuple-element.1246, s32[1024]{0:T(1024)S(1)} %pad_clamp_fusion.6), kind=kCustom, calls=%fused_computation.4.clone | custom fusion | bytes 14680960 | tf_op jit(solution)/shard_map/jit(_take)/gather | solution.py:129
  323.9 8.2 %multiply_convert_fusion = bf16[224,128,128]{2,1,0:T(8,128)(2,1)S(1)} fusion(bf16[224,128,128]{2,1,0:T(8,128)(2,1)} %gather_fusion.11, bf16[224,128,128]{2,1,0:T(8,128)(2,1)} %gather_fusion.9, f32[224]{0:T(256)S(1)} %compare_convert_fusion, pred[224]{0:T(512)(128)(4,1)S(1)} %get-tuple-element.947, pred[224]{0:T(512)(128)(4,1)S(1)} %get-tuple-element.958), kind=kOutput, calls=%fused_computation.124 | convolution fusion | flops 954204160 | bytes 22021440 | tf_op jit(solution)/shard_map/tsk,tsn->skn/dot_general | solution.py:130
  332.1 10.0 %multiply_convert_fusion.1 = bf16[224,128,128]{2,1,0:T(8,128)(2,1)} fusion(bf16[224,128,128]{2,1,0:T(8,128)(2,1)} %gather_fusion.7, bf16[224,128,128]{2,1,0:T(8,128)(2,1)} %gather_fusion.5, f32[224]{0:T(256)S(1)} %compare_convert_fusion.1, pred[224]{0:T(512)(128)(4,1)S(1)} %get-tuple-element.943, pred[224]{0:T(512)(128)(4,1)S(1)} %get-tuple-element.960), kind=kOutput, calls=%fused_computation.125 | convolution fusion | flops 954204160 | bytes 22021440 | tf_op jit(solution)/shard_map/tsk,tsn->skn/dot_general | solution.py:130
  342.2 9.6 %pad_maximum_fusion = bf16[32,7,2,128,128]{4,3,1,2,0:T(8,128)(2,1)} fusion(bf16[32,7,1,128,128]{4,3,1,2,0:T(8,128)(2,1)S(1)} %bitcast.188, bf16[32,7,1,128,128]{4,3,1,2,0:T(8,128)(2,1)} %bitcast.189), kind=kLoop, calls=%fused_computation.123 | loop fusion | flops 7340032 | bytes 29360128 | tf_op jit(solution)/shard_map/stack | solution.py:134
  351.8 8.2 %all-to-all-start = ((bf16[32,7,2,128,128]{4,3,1,2,0:T(8,128)(2,1)}), bf16[32,7,2,128,128]{4,3,1,2,0:T(8,128)(2,1)}, u32[]{:S(2)}, u32[]{:S(2)}) async-start(bf16[32,7,2,128,128]{4,3,1,2,0:T(8,128)(2,1)} %pad_maximum_fusion), calls=%async_computation.1 | async-start | bytes 29360128 | tf_op jit(solution)/shard_map/all_to_all | solution.py:136
  360.0 100.5 %while.62 = (s32[]{:T(128)}, f32[128,32,128]{2,1,0:T(8,128)}, s32[224]{0:T(256)S(1)}, s32[]{:T(128)}, bf16[224,128,128]{2,1,0:T(8,128)(2,1)}, /*index=5*/s32[224...) while((s32[]{:T(128)}, f32[128,32,128]{2,1,0:T(8,128)}, ...), condition=%wide.region_5.8_spmd.clone.clone, body=%wide.region_4.0_spmd.clone.clone.sunk | while | flops 205526272 | bytes 20976992 | solution.py:61
  361.7 3.1 fusion.165
  371.0 3.0 bitcast_add_fusion.4
  375.4 3.1 fusion.165
  384.7 3.7 bitcast_add_fusion.4
  389.9 3.2 fusion.165
  399.1 3.7 bitcast_add_fusion.4
  404.3 3.1 fusion.165
  413.5 3.7 bitcast_add_fusion.4
  418.7 3.2 fusion.165
  428.0 3.7 bitcast_add_fusion.4
  433.1 3.1 fusion.165
  442.4 3.7 bitcast_add_fusion.4
  447.6 3.2 fusion.165
  456.8 3.7 bitcast_add_fusion.4
  460.5 100.2 %while.63 = (s32[]{:T(128)}, f32[128,32,128]{2,1,0:T(8,128)}, s32[224]{0:T(256)S(1)}, s32[]{:T(128)}, bf16[224,128,128]{2,1,0:T(8,128)(2,1)}, /*index=5*/s32[224...) while((s32[]{:T(128)}, f32[128,32,128]{2,1,0:T(8,128)}, ...), condition=%wide.region_7.10_spmd.clone.clone, body=%wide.region_6.9_spmd.clone.clone.sunk | while | flops 205526272 | bytes 20976992 | solution.py:61
  462.0 3.2 fusion.171
  471.3 3.0 bitcast_add_fusion.5
  475.7 3.2 fusion.171
  485.0 3.6 bitcast_add_fusion.5
  490.1 3.2 fusion.171
  499.4 3.7 bitcast_add_fusion.5
  504.5 3.2 fusion.171
  513.8 3.6 bitcast_add_fusion.5
  519.0 3.2 fusion.171
  528.2 3.7 bitcast_add_fusion.5
  533.4 3.2 fusion.171
  542.7 3.6 bitcast_add_fusion.5
  547.8 3.2 fusion.171
  557.1 3.7 bitcast_add_fusion.5
  566.2 149.9 %all-to-all-done = bf16[32,7,2,128,128]{4,3,1,2,0:T(8,128)(2,1)} async-done(((bf16[32,7,2,128,128]{4,3,1,2,0:T(8,128)(2,1)}), bf16[32,7,2,128,128]{4,3,1,2,0:T(8,128)(2,1)}, u32[]{:S(2)}, u32[]{:S(2)}) %all-to-all-start) | async-done | bytes 14680096 | tf_op jit(solution)/shard_map/all_to_all | solution.py:136
  716.1 8.9 %convert_reduce_fusion = f32[7,2,128,128]{3,2,0,1:T(8,128)S(1)} fusion(bf16[32,7,2,128,128]{4,3,1,2,0:T(8,128)(2,1)} %all-to-all-done), kind=kLoop, calls=%fused_computation.122 | loop fusion | flops 14450688 | bytes 15597568 | tf_op jit(solution)/shard_map/reduce_sum | solution.py:137
  (250 shorter events, 236.1 us)
Async XLA Ops:
  7.2 29.2 %all-gather.6.cloned.1.call-start = ((), (), s32[]{:S(2)}) async-start(), calls=%async_computation.3 | async-start | bytes 1179648 | tf_op jit(solution)/shard_map/all_gather | solution.py:76
  8.9 120.6 %all-gather.8.cloned.1.call-start = ((), (), s32[]{:S(2)}) async-start(), calls=%async_computation.4 | async-start | bytes 7569408 | tf_op jit(solution)/shard_map/all_gather | solution.py:82
  9.7 212.9 %all-gather.4.cloned.1.call-start = ((), (), s32[]{:S(2)}) async-start(), calls=%async_computation.2 | async-start | bytes 7569408 | tf_op jit(solution)/shard_map/all_gather | solution.py:81
  46.8 82.7 %copy-start.2 = (s32[1,224]{1,0:T(1,128)S(1)}, s32[1,224]{1,0:T(1,128)}, u32[]{:S(2)}) copy-start(s32[1,224]{1,0:T(1,128)} %param.36) | copy-start | bytes 2692
  46.8 82.7 %copy-start.3 = (s32[1,224]{1,0:T(1,128)S(1)}, s32[1,224]{1,0:T(1,128)}, u32[]{:S(2)}) copy-start(s32[1,224]{1,0:T(1,128)} %param.35) | copy-start | bytes 2692
  129.5 93.0 %copy-start = (s32[1,224]{1,0:T(1,128)S(1)}, s32[1,224]{1,0:T(1,128)}, u32[]{:S(2)}) copy-start(s32[1,224]{1,0:T(1,128)} %param.33) | copy-start | bytes 2692
  129.5 93.0 %copy-start.1 = (s32[1,224]{1,0:T(1,128)S(1)}, s32[1,224]{1,0:T(1,128)}, u32[]{:S(2)}) copy-start(s32[1,224]{1,0:T(1,128)} %param.32) | copy-start | bytes 2692
  351.8 364.4 %all-to-all-start = ((bf16[32,7,2,128,128]{4,3,1,2,0:T(8,128)(2,1)}), bf16[32,7,2,128,128]{4,3,1,2,0:T(8,128)(2,1)}, u32[]{:S(2)}, u32[]{:S(2)}) async-start(bf16[32,7,2,128,128]{4,3,1,2,0:T(8,128)(2,1)} %pad_maximum_fusion), calls=%async_computation.1 | async-start | bytes 29360128 | tf_op jit(solution)/shard_map/all_to_all | solution.py:136
  359.9 366.0 %reduce-scatter.2.cloned.1.call-start = ((), (), s32[]{:S(2)}) async-start(), calls=%async_computation.5 | async-start | bytes 1179648 | tf_op jit(solution)/shard_map/reduce_scatter | solution.py:113
Sparse Core Ops, SparseCore 0:
  10.4 25.8 all-gather.5
  38.9 90.5 all-gather.7
  132.1 90.3 all-gather.3
  565.0 33.7 reduce-scatter.1
where the time goes:
time: 740 us; the launch traced here: 733 us
  waiting for transfers between devices  251 us (34%)
  matrix products  236 us (32%)
  local copies, waits for them, and re-layouts  176 us (24%)
  other arithmetic  45.2 us (6%)
  between operations  15.4 us (2%)
  starting transfers between devices  8.33 us (1%)
    all_to_all x1, waiting for transfers between devices, on_device(): lax.all_to_all(shaped, 'seq', split_axis=0, concat_axis=0, tiled=True)  150 us
    dot_general x28, matrix products, place_split(): jnp.einsum(form, rest_part, table, preferred_element_type=jnp.float32)  89 us
    all_gather x1, waiting for transfers between devices, on_device(): up_all = lax.all_gather(up_blocks, 'seq', axis=1, tiled=True)  74.4 us
    convert_element_type x28, local copies, waits for them, and re-layouts, place_split(): rest_part = (products - high_part.astype(jnp.float32)).astype(jnp.bfloat16)  51.1 us
    convert_element_type x28, local copies, waits for them, and re-layouts, place_split(): high_part = products.astype(jnp.bfloat16)  50.9 us
    dot_general x14, matrix products, return_one_group(): jnp.einsum('tsn,skn->tsk', picked, chosen, preferred_element_type=jnp.flo...  44.2 us
    dot_general x14, matrix products, project_one_group(): jnp.einsum('tsk,skn->tsn', picked, chosen, preferred_element_type=jnp.flo...  43.9 us
    dot_general x28, matrix products, place_split(): jnp.einsum(form, high_part, table, preferred_element_type=jnp.float32)  41 us
  transfers between devices with their start and end apart: 5, of which 4 were waited for; matrix products, arithmetic and copies ran while one was open for 45% of the time, Pallas kernels for 0%

commit v1 on v0

v1 whole, which is shorter than its diff:
```python
import math

import jax
import jax.numpy as jnp
from jax import lax
from jax.experimental import pallas as pl
from jax.experimental.pallas import tpu as pltpu
from jax.sharding import Mesh
from jax.sharding import PartitionSpec as P

AXES = ("xh", "xl", "z", "y", "core")
BS = 128
UNROLL = 4


def tile(index):
    return pl.ds(pl.multiple_of(index * BS, BS), BS)


def forward_kernel(sched, counts, which, x_ref, w_ref, own_ref, send_ref, acc_ref):
    width = own_ref.shape[2]
    core = which[0]
    for matrix in range(2):
        acc_ref[...] = jnp.zeros_like(acc_ref)

        def step(trip, carry):
            products = []
            for u in range(UNROLL):
                q = trip * UNROLL + u
                x = x_ref[:, tile(sched[0, matrix, q])]
                w = w_ref[sched[2, matrix, q]]
                products.append(jnp.dot(x, w, preferred_element_type=jnp.float32))
            for u in range(UNROLL):
                col = tile(sched[1, matrix, trip * UNROLL + u])
                acc_ref[:, col] = acc_ref[:, col] + products[u]
            return carry

        lax.fori_loop(0, pl.cdiv(counts[matrix], UNROLL), step, 0)
        own_ref[matrix] = acc_ref[tile(core), :width]
        send_ref[matrix] = acc_ref[tile(1 - core), :width]


def input_kernel(sched, counts, which, own_g_ref, mate_g_ref, w_ref, own_ref, send_ref, acc_ref, g_ref):
    width = own_ref.shape[1]
    core = which[0]
    acc_ref[...] = jnp.zeros_like(acc_ref)
    for matrix in range(2):
        g_ref[tile(core), :] = own_g_ref[matrix]
        g_ref[tile(1 - core), :] = mate_g_ref[matrix]

        def step(trip, carry):
            products = []
            for u in range(UNROLL):
                q = trip * UNROLL + u
                g = g_ref[:, tile(sched[4, matrix, q])]
                w = w_ref[sched[2, matrix, q]]
                products.append(
                    lax.dot_general(g, w, (((1,), (1,)), ((), ())), preferred_element_type=jnp.float32)
                )
            for u in range(UNROLL):
                row = tile(sched[3, matrix, trip * UNROLL + u])
                acc_ref[:, row] = acc_ref[:, row] + products[u]
            return carry

        lax.fori_loop(0, pl.cdiv(counts[matrix], UNROLL), step, 0)
    own_ref[...] = acc_ref[tile(core), :width].astype(own_ref.dtype)
    send_ref[...] = acc_ref[tile(1 - core), :width].astype(send_ref.dtype)


def weight_kernel(sched, counts, which, own_g_ref, mate_g_ref, xt_ref, out_ref, g_ref):
    core = which[0]
    out_ref[...] = jnp.zeros_like(out_ref)
    for matrix in range(2):
        g_ref[tile(core), :] = own_g_ref[matrix]
        g_ref[tile(1 - core), :] = mate_g_ref[matrix]
        live = counts[matrix]

        def step(trip, carry):
            for u in range(UNROLL):
                q = trip * UNROLL + u
                xt = xt_ref[tile(sched[0, matrix, q]), :]
                g = g_ref[:, tile(sched[4, matrix, q])]
                term = jnp.dot(xt, g, preferred_element_type=jnp.float32)
                term = jnp.where(q < live, term, 0.0)
                out_ref[sched[2, matrix, q]] = term.astype(out_ref.dtype)
            return carry

        lax.fori_loop(0, pl.cdiv(live, UNROLL), step, 0)


def call(kernel, out_shape, scratch, scalars, arrays, flops):
    spec = pl.BlockSpec(memory_space=pltpu.VMEM)
    return pl.pallas_call(
        kernel,
        out_shape=out_shape,
        grid_spec=pltpu.PrefetchScalarGridSpec(
            num_scalar_prefetch=len(scalars),
            grid=(),
            in_specs=[spec] * len(arrays),
            out_specs=jax.tree.map(lambda _: spec, out_shape),
            scratch_shapes=scratch,
        ),
        compiler_params=pltpu.CompilerParams(vmem_limit_bytes=56 * 1024 * 1024),
        cost_estimate=pl.CostEstimate(flops=flops, transcendentals=0, bytes_accessed=10_000_000),
    )(*scalars, *arrays)


def on_device(
    tokens,
    hidden_grad,
    gate_blocks,
    up_blocks,
    gate_rows,
    gate_cols,
    gate_count,
    up_rows,
    up_cols,
    up_count,
):
    sizes = {name: lax.axis_size(name) for name in AXES}
    side = lax.axis_index("xh")
    core = lax.axis_index("core")
    home = side == core
    tok_rows = tokens.shape[0]
    per_owner = gate_blocks.shape[1]
    capacity = gate_rows.shape[1]
    width = hidden_grad.shape[1]
    col_blocks = width // BS

    def swap(value):
        return lax.ppermute(value, ("xh", "core"), [(0, 0), (1, 2), (2, 1), (3, 3)])

    def mate(value):
        return lax.ppermute(value, "core", [(0, 1), (1, 0)])

    stored = swap(jnp.concatenate([gate_blocks[0], up_blocks[0]], axis=0))
    blocks = lax.all_gather(stored, ("xl", "z"), axis=0, tiled=True)

    packed = jnp.concatenate(
        [gate_rows[0], up_rows[0], gate_cols[0], up_cols[0], gate_count, up_count]
    )
    packed = jnp.where(home, packed, mate(packed))
    half = capacity // 2
    tables = packed[: 4 * capacity].reshape(2, 2, 2, half)
    tables = lax.dynamic_index_in_dim(tables, core, 2, keepdims=False)
    live = jnp.clip(packed[4 * capacity :] - core * half, 0, half).astype(jnp.int32)
    slot = jnp.arange(half, dtype=jnp.int32)
    used = slot[None, :] < live[:, None]
    place = (slot // per_owner) * (2 * per_owner) + slot % per_owner
    place = jnp.stack([place, place + per_owner])
    row_blocks = sizes["y"] * sizes["core"] * tokens.shape[1] // BS
    sched = jnp.stack(
        [
            tables[0],
            jnp.where(used, tables[1], col_blocks),
            place,
            jnp.where(used, tables[0], row_blocks),
            tables[1],
        ]
    ).astype(jnp.int32)
    which = core.astype(jnp.int32).reshape(1)

    other = lax.ppermute(tokens, "xh", [(0, 1), (1, 0)])
    pair = jnp.concatenate(
        [jnp.where(side == 0, tokens, other), jnp.where(side == 0, other, tokens)], axis=0
    )
    ny = sizes["y"]
    yid = lax.axis_index("y")
    from_y = [pair] + [
        lax.ppermute(pair, "y", [(i, (i + s) % ny) for i in range(ny)]) for s in range(1, ny)
    ]
    from_y = jnp.stack(from_y)
    from_y = jnp.stack(
        [
            lax.dynamic_index_in_dim(from_y, (yid - i) % ny, 0, keepdims=False)
            for i in range(ny)
        ]
    )
    from_mate = mate(from_y)
    by_core = jnp.stack(
        [jnp.where(core == 0, from_y, from_mate), jnp.where(core == 0, from_mate, from_y)], axis=1
    )
    x = by_core.transpose(2, 0, 1, 3).reshape(2 * tok_rows, row_blocks * BS)
    xt = x.T

    scalars = (sched, live, which)
    pre = jax.ShapeDtypeStruct((2, tok_rows, width), jnp.float32)
    flops = half * 2 * 2 * tok_rows * BS * BS * 2
    own, send = call(
        forward_kernel,
        (pre, pre),
        [pltpu.VMEM((2 * tok_rows, width + BS), jnp.float32)],
        scalars,
        (x, blocks),
        flops,
    )
    summed = own + mate(send)
    gate, up = summed[0], summed[1]
    upstream = swap(hidden_grad).astype(jnp.float32)
    sigma = jax.nn.sigmoid(gate)
    activated = gate * sigma
    slope = sigma * (1.0 + gate * (1.0 - sigma))
    hidden = (activated * up).astype(jnp.bfloat16)
    grads = jnp.stack(
        [(upstream * up * slope).astype(jnp.bfloat16), (upstream * activated).astype(jnp.bfloat16)]
    )
    mate_grads = mate(grads)
    hidden = swap(hidden)

    share = jax.ShapeDtypeStruct((tok_rows, row_blocks * BS), jnp.bfloat16)
    own_in, send_in = call(
        input_kernel,
        (share, share),
        [
            pltpu.VMEM((2 * tok_rows, (row_blocks + 1) * BS), jnp.float32),
            pltpu.VMEM((2 * tok_rows, width), jnp.bfloat16),
        ],
        scalars,
        (grads, mate_grads, blocks),
        flops,
    )
    panel_input = (own_in.astype(jnp.float32) + mate(send_in).astype(jnp.float32)).astype(jnp.bfloat16)
    input_grad = swap(lax.psum_scatter(panel_input, ("y", "xh"), scatter_dimension=1, tiled=True))

    terms = call(
        weight_kernel,
        jax.ShapeDtypeStruct(blocks.shape, jnp.bfloat16),
        [pltpu.VMEM((2 * tok_rows, width), jnp.bfloat16)],
        scalars,
        (grads, mate_grads, xt),
        flops,
    )
    terms = lax.psum_scatter(terms, ("xl", "z"), scatter_dimension=0, tiled=True)
    scale = 1.0 / math.sqrt(tok_rows * sizes["xh"] * sizes["xl"] * sizes["z"])
    terms = swap((terms.astype(jnp.float32) * scale).astype(jnp.bfloat16))
    return hidden, input_grad, terms[None, :per_owner], terms[None, per_owner:]


def solution(mesh):
    shape = mesh.devices.shape
    fine = Mesh(mesh.devices.reshape(2, 2, shape[0] // 4, shape[1] // 2, 2), AXES)
    seq, hid = ("xh", "xl", "z"), ("y", "core")
    placed = (
        P(seq, hid),
        P(seq, hid),
        P(hid, seq, None, None),
        P(hid, seq, None, None),
        P(hid, None),
        P(hid, None),
        P(hid),
        P(hid, None),
        P(hid, None),
        P(hid),
    )
    return jax.shard_map(
        on_device,
        mesh=fine,
        in_specs=placed,
        out_specs=(P(seq, hid), P(seq, hid), P(hid, seq, None, None), P(hid, seq, None, None)),
        check_vma=False,
    )
```

time: 740 us -> 353 us (0.48)
  the two profiles are of different devices: /device:TPU:179 before, /device:TPU:1 now
where the time goes in v1:
time: 353 us; the launch traced here: 354 us
  waiting for transfers between devices  225 us (64%)
  starting transfers between devices  72.8 us (21%)
  Pallas kernels  20.3 us (6%)
  between operations  15.3 us (4%)
  local copies, waits for them, and re-layouts  10.7 us (3%)
  other arithmetic  10.4 us (3%)
    reduce_scatter x1, waiting for transfers between devices, on_device(): lax.psum_scatter(panel_input, ('y', 'xh'), scatter_dimension=1, tiled=True)  69.5 us
    reduce_scatter x1, waiting for transfers between devices, on_device(): lax.psum_scatter(terms, ('xl', 'z'), scatter_dimension=0, tiled=True)  63.1 us
    all_gather x1, waiting for transfers between devices, on_device(): blocks = lax.all_gather(stored, ('xl', 'z'), axis=0, tiled=True)  56.7 us
    ppermute x5, starting transfers between devices, swap(): return lax.ppermute(value, ('xh', 'core'), [(0, 0), (1, 2), (2, 1), (3, 3)])  48.7 us
    pallas_call x3, Pallas kernels, call(): pl.pallas_call(kernel, out_shape=out_shape, grid_spec=pltpu.PrefetchScala...  20.3 us
    ppermute x5, starting transfers between devices, mate(): return lax.ppermute(value, 'core', [(0, 1), (1, 0)])  20 us
    ppermute x3, waiting for transfers between devices, on_device(): lax.ppermute(pair, 'y', [(i, (i + s) % ny) for i in range(ny)])  14.2 us
    ppermute x5, waiting for transfers between devices, swap(): return lax.ppermute(value, ('xh', 'core'), [(0, 0), (1, 2), (2, 1), (3, 3)])  13.3 us
  transfers between devices with their start and end apart: 17, of which 13 were waited for; matrix products, arithmetic and copies ran while one was open for 4% of the time, Pallas kernels for 2%

profile of v1, /device:TPU:1, one launch (start us, length us, event | category | flops | bytes accessed | tf_op | source)
XLA Modules:
  0.0 354.4 jit_solution(16309657586157301933)
XLA Ops:
  7.2 0.0 all-gather.2.cloned.1.call-start
  7.2 1.1 pad_maximum_fusion.3
  8.3 6.0 %collective-permute-start.6 = (bf16[14,128,128]{2,1,0:T(8,128)(2,1)S(1)}, bf16[14,128,128]{2,1,0:T(8,128)(2,1)S(1)}, u32[]{:S(2)}, u32[]{:S(2)}) collective-permute-start(bf16[14,128,128]{2,1,0:T(8,128)(2,1)S(1)} %pad_maximum_fusion.3), channel_id=1, source_target_pairs={{0,0},{1,128},{128,1},{129,129},{2,2},{3,130},{130,3},{131,131},{4... | collective-permute-start | bytes 1376264 | tf_op jit(solution)/shard_map/ppermute | solution.py:131
  14.4 6.1 %collective-permute-done.6 = bf16[14,128,128]{2,1,0:T(8,128)(2,1)S(1)} collective-permute-done((bf16[14,128,128]{2,1,0:T(8,128)(2,1)S(1)}, bf16[14,128,128]{2,1,0:T(8,128)(2,1)S(1)}, u32[]{:S(2)}, u32[]{:S(2)}) %collective-permute-start.6) | collective-permute-done | bytes 458784 | tf_op jit(solution)/shard_map/ppermute | solution.py:131
  20.5 0.8 copy-done.3
  21.3 0.0 all-gather.2.cloned.1.call-update
  21.3 0.0 reduce-scatter.5.cloned.1.call-start
  21.3 0.1 collective-permute-start.1
  22.7 0.8 concatenate.9
  23.5 3.6 %collective-permute-start = (s32[898]{0:T(1024)S(1)}, s32[898]{0:T(1024)S(1)}, u32[]{:S(2)}, u32[]{:S(2)}) collective-permute-start(s32[898]{0:T(1024)S(1)} %concatenate.9), channel_id=1, source_target_pairs={{0,1},{1,0},{2,3},{3,2},{4,5},{5,4},{6,7},{7,6},{8,9},{9,8},{10,11... | collective-permute-start | bytes 10784 | tf_op jit(solution)/shard_map/ppermute | solution.py:134
  27.2 1.0 collective-permute-done.1
  28.2 0.9 broadcast_select_fusion.1
  29.1 2.8 collective-permute-start.4
  31.9 0.3 collective-permute-start.3
  32.3 0.7 collective-permute-start.2
  33.1 0.0 collective-permute-done
  33.1 0.1 reshape.145
  33.2 4.5 %collective-permute-done.4 = bf16[256,512]{1,0:T(8,128)(2,1)S(1)} collective-permute-done((bf16[256,512]{1,0:T(8,128)(2,1)S(1)}, bf16[256,512]{1,0:T(8,128)(2,1)S(1)}, u32[]{:S(2)}, u32[]{:S(2)}) %collective-permute-start.4) | collective-permute-done | bytes 262176 | tf_op jit(solution)/shard_map/ppermute | solution.py:170
  37.7 2.4 collective-permute-done.3
  40.1 7.3 %collective-permute-done.2 = bf16[256,512]{1,0:T(8,128)(2,1)S(1)} collective-permute-done((bf16[256,512]{1,0:T(8,128)(2,1)S(1)}, bf16[256,512]{1,0:T(8,128)(2,1)S(1)}, u32[]{:S(2)}, u32[]{:S(2)}) %collective-permute-start.2) | collective-permute-done | bytes 262176 | tf_op jit(solution)/shard_map/ppermute | solution.py:170
  47.4 0.1 pad_maximum_fusion
  47.5 0.1 constant_dynamic-slice_fusion.4
  47.6 0.1 pad_maximum_fusion.1
  47.8 0.5 collective-permute-start.5
  48.3 0.0 copy-start.5
  48.3 0.1 constant_dynamic-update-slice_fusion.3
  48.4 0.1 constant_dynamic-update-slice_fusion.1
  48.5 2.1 collective-permute-done.5
  50.5 0.2 select_bitcast_fusion.1
  50.7 1.6 maximum_bitcast_fusion
  52.3 2.8 copy.20
  55.1 3.0 copy.21.x_ref
  58.2 56.7 %all-gather.2.cloned.1.call-done.w_ref = bf16[224,128,128]{2,1,0:T(8,128)(2,1)} async-done(((bf16[14,128,128]{2,1,0:T(8,128)(2,1)}), bf16[224,128,128]{2,1,0:T(8,128)(2,1)}) %all-gather.2.cloned.1.call-update) | async-done | bytes 7340048 | tf_op jit(solution)/shard_map/all_gather | solution.py:137
  114.8 7.0 %shard_map.129 = (f32[2,128,1792]{2,1,0:T(8,128)}, f32[2,128,1792]{2,1,0:T(8,128)}) custom-call(s32[5,2,112]{2,1,0:T(2,128)} %copy-done.4, s32[2]{0:T(128)} %copy-done.5, s32[1]{0:T(128)} %bitcast.7.which, bf16[256,4096]{1,0:T(8,128)(2,1)} %copy.21.x_ref, bf16[224,128,128]{2,1,0:T(8,128)(2,1)} %all-gather.2.cloned.1.call-done.w_ref), custom_call_target="tpu_custom_call" | custom-call | flops 1879048192 | bytes 10000000 | tf_op jit(solution)/shard_map/pallas_call | solution.py:93
  121.8 5.7 %collective-permute-start.7 = (f32[2,128,1792]{2,1,0:T(8,128)}, f32[2,128,1792]{2,1,0:T(8,128)S(1)}, u32[]{:S(2)}, u32[]{:S(2)}) collective-permute-start(f32[2,128,1792]{2,1,0:T(8,128)} %get-tuple-element.9), channel_id=1, source_target_pairs={{0,1},{1,0},{2,3},{3,2},{4,5},{5,4},{6,7},{7,6},{8,9},{9,8},{10,11... | collective-permute-start | bytes 5505032 | tf_op jit(solution)/shard_map/ppermute | solution.py:134
  127.5 10.1 %collective-permute-start.9 = (bf16[128,1792]{1,0:T(8,128)(2,1)S(1)}, bf16[128,1792]{1,0:T(8,128)(2,1)S(1)}, u32[]{:S(2)}, u32[]{:S(2)}) collective-permute-start(bf16[128,1792]{1,0:T(8,128)(2,1)S(1)} %copy-done.6), channel_id=1, source_target_pairs={{0,0},{1,128},{128,1},{129,129},{2,2},{3,130},{130,3},{131,131},{4... | collective-permute-start | bytes 1376264 | tf_op jit(solution)/shard_map/ppermute | solution.py:131
  137.6 0.0 collective-permute-done.7
  137.6 1.8 add.119
  139.4 4.3 %collective-permute-done.9 = bf16[128,1792]{1,0:T(8,128)(2,1)S(1)} collective-permute-done((bf16[128,1792]{1,0:T(8,128)(2,1)S(1)}, bf16[128,1792]{1,0:T(8,128)(2,1)S(1)}, u32[]{:S(2)}, u32[]{:S(2)}) %collective-permute-start.9) | collective-permute-done | bytes 458784 | tf_op jit(solution)/shard_map/ppermute | solution.py:131
  143.7 0.6 fusion.5
  144.4 0.1 pad_maximum_fusion.2.own_g_ref
  144.5 0.1 collective-permute-start.10
  144.6 2.5 collective-permute-done.10.mate_g_ref
  147.1 0.9 copy-done.2
  148.0 7.0 %shard_map.131 = bf16[224,128,128]{2,1,0:T(8,128)(2,1)} custom-call(s32[5,2,112]{2,1,0:T(2,128)} %copy-done.4, s32[2]{0:T(128)} %copy-done.5, s32[1]{0:T(128)} %bitcast.7.which, bf16[2,128,1792]{2,1,0:T(8,128)(2,1)} %copy-done.1, bf16[2,128,1792]{2,1,0:T(8,128)(2,1)} %copy-done.2, bf16[4096,256]{1,0:T(8,128)(2,1)} %bitcast.62), custom_call_target="tpu_custom_call" | custom-call | flops 1879048192 | bytes 10000000 | tf_op jit(solution)/shard_map/pallas_call | solution.py:93
  154.9 0.0 reduce-scatter.5.cloned.1.call-update
  155.0 0.0 reduce-scatter.3.cloned.1.call-start
  155.0 6.3 %shard_map.130 = (bf16[128,4096]{1,0:T(8,128)(2,1)}, bf16[128,4096]{1,0:T(8,128)(2,1)}) custom-call(s32[5,2,112]{2,1,0:T(2,128)} %copy-done.4, s32[2]{0:T(128)} %copy-done.5, s32[1]{0:T(128)} %bitcast.7.which, bf16[2,128,1792]{2,1,0:T(8,128)(2,1)} %copy-done.1, bf16[2,128,1792]{2,1,0:T(8,128)(2,1)} %copy-done.2, ...), custom_call_target="tpu_custom_call" | custom-call | flops 1879048192 | bytes 10000000 | tf_op jit(solution)/shard_map/pallas_call | solution.py:93
  161.3 10.1 %collective-permute-start.11 = (bf16[128,4096]{1,0:T(8,128)(2,1)}, bf16[128,4096]{1,0:T(8,128)(2,1)S(1)}, u32[]{:S(2)}, u32[]{:S(2)}) collective-permute-start(bf16[128,4096]{1,0:T(8,128)(2,1)} %get-tuple-element.11), channel_id=1, source_target_pairs={{0,1},{1,0},{2,3},{3,2},{4,5},{5,4},{6,7},{7,6},{8,9},{9,8},{10,11... | collective-permute-start | bytes 3145736 | tf_op jit(solution)/shard_map/ppermute | solution.py:134
  171.5 2.5 collective-permute-done.11
  174.0 2.5 add_convert_fusion
  176.4 0.0 reduce-scatter.3.cloned.1.call-update
  176.5 17.3 %collective-permute-start.8 = (bf16[128,1792]{1,0:T(8,128)(2,1)S(1)}, bf16[128,1792]{1,0:T(8,128)(2,1)S(1)}, u32[]{:S(2)}, u32[]{:S(2)}) collective-permute-start(bf16[128,1792]{1,0:T(8,128)(2,1)S(1)} %get-tuple-element.16), channel_id=1, source_target_pairs={{0,0},{1,128},{128,1},{129,129},{2,2},{3,130},{130,3},{131,131},{4... | collective-permute-start | bytes 1376264 | tf_op jit(solution)/shard_map/ppermute | solution.py:131
  193.8 63.1 %reduce-scatter.5.cloned.1.call-done = bf16[14,128,128]{2,1,0:T(8,128)(2,1)} async-done(((bf16[224,128,128]{2,1,0:T(8,128)(2,1)}), bf16[14,128,128]{2,1,0:T(8,128)(2,1)}) %reduce-scatter.5.cloned.1.call-update) | async-done | bytes 458768 | tf_op jit(solution)/shard_map/reduce_scatter | solution.py:233
  256.9 1.1 multiply_convert_fusion
  258.0 8.9 %collective-permute-start.13 = (bf16[14,128,128]{2,1,0:T(8,128)(2,1)S(1)}, bf16[14,128,128]{2,1,0:T(8,128)(2,1)S(1)}, u32[]{:S(2)}, u32[]{:S(2)}) collective-permute-start(bf16[14,128,128]{2,1,0:T(8,128)(2,1)S(1)} %multiply_convert_fusion), channel_id=1, source_target_pairs={{0,0},{1,128},{128,1},{129,129},{2,2},{3,130},{130,3},{131,131},{4... | collective-permute-start | bytes 1376264 | tf_op jit(solution)/shard_map/ppermute | solution.py:131
  266.9 69.5 %reduce-scatter.3.cloned.1.call-done = bf16[128,512]{1,0:T(8,128)(2,1)} async-done(((bf16[128,4096]{1,0:T(8,128)(2,1)}), bf16[128,512]{1,0:T(8,128)(2,1)}) %reduce-scatter.3.cloned.1.call-update) | async-done | bytes 131088 | tf_op jit(solution)/shard_map/reduce_scatter | solution.py:223
  336.4 6.4 %collective-permute-start.12 = (bf16[128,512]{1,0:T(8,128)(2,1)}, bf16[128,512]{1,0:T(8,128)(2,1)S(1)}, u32[]{:S(2)}, u32[]{:S(2)}) collective-permute-start(bf16[128,512]{1,0:T(8,128)(2,1)} %reduce-scatter.3.cloned.1.call-done), channel_id=1, source_target_pairs={{0,0},{1,128},{128,1},{129,129},{2,2},{3,130},{130,3},{131,131},{4... | collective-permute-start | bytes 393224 | tf_op jit(solution)/shard_map/ppermute | solution.py:131
  342.8 0.0 collective-permute-done.8
  342.8 2.8 collective-permute-done.12
  345.6 0.0 collective-permute-done.13
  345.6 0.8 slice_bitcast_fusion.2
  346.4 0.8 copy.33
  347.2 0.7 copy.34
  (19 shorter events, 0.1 us)
Async XLA Ops:
  7.2 107.7 %all-gather.2.cloned.1.call-start = ((), (), s32[]{:S(2)}) async-start(), calls=%async_computation.2 | async-start | bytes 7798784 | tf_op jit(solution)/shard_map/all_gather | solution.py:137
  8.3 12.2 %collective-permute-start.6 = (bf16[14,128,128]{2,1,0:T(8,128)(2,1)S(1)}, bf16[14,128,128]{2,1,0:T(8,128)(2,1)S(1)}, u32[]{:S(2)}, u32[]{:S(2)}) collective-permute-start(bf16[14,128,128]{2,1,0:T(8,128)(2,1)S(1)} %pad_maximum_fusion.3), channel_id=1, source_target_pairs={{0,0},{1,128},{128,1},{129,129},{2,2},{3,130},{130,3},{131,131},{4... | collective-permute-start | bytes 1376264 | tf_op jit(solution)/shard_map/ppermute | solution.py:131
  20.5 0.8 copy-start.3
  21.3 235.6 %reduce-scatter.5.cloned.1.call-start = ((), (), s32[]{:S(2)}) async-start(), calls=%async_computation.4 | async-start | bytes 7798784 | tf_op jit(solution)/shard_map/reduce_scatter | solution.py:233
  21.3 6.8 %collective-permute-start.1 = (bf16[128,512]{1,0:T(8,128)(2,1)}, bf16[128,512]{1,0:T(8,128)(2,1)S(1)}, u32[]{:S(2)}, u32[]{:S(2)}) collective-permute-start(bf16[128,512]{1,0:T(8,128)(2,1)} %param.10), channel_id=1, source_target_pairs={{0,128},{128,0},{1,129},{129,1},{2,130},{130,2},{3,131},{131,3},{4... | collective-permute-start | bytes 393224 | tf_op jit(solution)/shard_map/ppermute | solution.py:163
  23.5 9.5 %collective-permute-start = (s32[898]{0:T(1024)S(1)}, s32[898]{0:T(1024)S(1)}, u32[]{:S(2)}, u32[]{:S(2)}) collective-permute-start(s32[898]{0:T(1024)S(1)} %concatenate.9), channel_id=1, source_target_pairs={{0,1},{1,0},{2,3},{3,2},{4,5},{5,4},{6,7},{7,6},{8,9},{9,8},{10,11... | collective-permute-start | bytes 10784 | tf_op jit(solution)/shard_map/ppermute | solution.py:134
  29.1 8.6 %collective-permute-start.4 = (bf16[256,512]{1,0:T(8,128)(2,1)S(1)}, bf16[256,512]{1,0:T(8,128)(2,1)S(1)}, u32[]{:S(2)}, u32[]{:S(2)}) collective-permute-start(bf16[256,512]{1,0:T(8,128)(2,1)S(1)} %get-tuple-element.24), channel_id=1, source_target_pairs={{0,6},{2,0},{4,2},{6,4},{1,7},{3,1},{5,3},{7,5},{8,14},{10,8},{12,... | collective-permute-start | bytes 786440 | tf_op jit(solution)/shard_map/ppermute | solution.py:170
  31.9 8.2 %collective-permute-start.3 = (bf16[256,512]{1,0:T(8,128)(2,1)S(1)}, bf16[256,512]{1,0:T(8,128)(2,1)S(1)}, u32[]{:S(2)}, u32[]{:S(2)}) collective-permute-start(bf16[256,512]{1,0:T(8,128)(2,1)S(1)} %get-tuple-element.24), channel_id=1, source_target_pairs={{0,4},{2,6},{4,0},{6,2},{1,5},{3,7},{5,1},{7,3},{8,12},{10,14},{12... | collective-permute-start | bytes 786440 | tf_op jit(solution)/shard_map/ppermute | solution.py:170
  32.3 15.1 %collective-permute-start.2 = (bf16[256,512]{1,0:T(8,128)(2,1)S(1)}, bf16[256,512]{1,0:T(8,128)(2,1)S(1)}, u32[]{:S(2)}, u32[]{:S(2)}) collective-permute-start(bf16[256,512]{1,0:T(8,128)(2,1)S(1)} %get-tuple-element.24), channel_id=1, source_target_pairs={{0,2},{2,4},{4,6},{6,0},{1,3},{3,5},{5,7},{7,1},{8,10},{10,12},{12... | collective-permute-start | bytes 786440 | tf_op jit(solution)/shard_map/ppermute | solution.py:170
  47.8 2.8 collective-permute-start.5
  48.3 2.4 copy-start.5
  48.5 2.3 copy-start.4
  55.1 3.0 copy-start
  114.8 12.7 %copy-start.6 = (bf16[128,1792]{1,0:T(8,128)(2,1)S(1)}, bf16[128,1792]{1,0:T(8,128)(2,1)}, u32[]{:S(2)}) copy-start(bf16[128,1792]{1,0:T(8,128)(2,1)} %param.11) | copy-start | bytes 1376260
  121.8 15.8 %collective-permute-start.7 = (f32[2,128,1792]{2,1,0:T(8,128)}, f32[2,128,1792]{2,1,0:T(8,128)S(1)}, u32[]{:S(2)}, u32[]{:S(2)}) collective-permute-start(f32[2,128,1792]{2,1,0:T(8,128)} %get-tuple-element.9), channel_id=1, source_target_pairs={{0,1},{1,0},{2,3},{3,2},{4,5},{5,4},{6,7},{7,6},{8,9},{9,8},{10,11... | collective-permute-start | bytes 5505032 | tf_op jit(solution)/shard_map/ppermute | solution.py:134
  127.5 16.3 %collective-permute-start.9 = (bf16[128,1792]{1,0:T(8,128)(2,1)S(1)}, bf16[128,1792]{1,0:T(8,128)(2,1)S(1)}, u32[]{:S(2)}, u32[]{:S(2)}) collective-permute-start(bf16[128,1792]{1,0:T(8,128)(2,1)S(1)} %copy-done.6), channel_id=1, source_target_pairs={{0,0},{1,128},{128,1},{129,129},{2,2},{3,130},{130,3},{131,131},{4... | collective-permute-start | bytes 1376264 | tf_op jit(solution)/shard_map/ppermute | solution.py:131
  144.5 2.6 copy-start.1
  144.5 2.6 collective-permute-start.10
  147.0 0.9 copy-start.2
  155.0 181.4 %reduce-scatter.3.cloned.1.call-start = ((), (), s32[]{:S(2)}) async-start(), calls=%async_computation.3 | async-start | bytes 1179648 | tf_op jit(solution)/shard_map/reduce_scatter | solution.py:223
  161.3 12.6 %collective-permute-start.11 = (bf16[128,4096]{1,0:T(8,128)(2,1)}, bf16[128,4096]{1,0:T(8,128)(2,1)S(1)}, u32[]{:S(2)}, u32[]{:S(2)}) collective-permute-start(bf16[128,4096]{1,0:T(8,128)(2,1)} %get-tuple-element.11), channel_id=1, source_target_pairs={{0,1},{1,0},{2,3},{3,2},{4,5},{5,4},{6,7},{7,6},{8,9},{9,8},{10,11... | collective-permute-start | bytes 3145736 | tf_op jit(solution)/shard_map/ppermute | solution.py:134
  176.5 166.3 %collective-permute-start.8 = (bf16[128,1792]{1,0:T(8,128)(2,1)S(1)}, bf16[128,1792]{1,0:T(8,128)(2,1)S(1)}, u32[]{:S(2)}, u32[]{:S(2)}) collective-permute-start(bf16[128,1792]{1,0:T(8,128)(2,1)S(1)} %get-tuple-element.16), channel_id=1, source_target_pairs={{0,0},{1,128},{128,1},{129,129},{2,2},{3,130},{130,3},{131,131},{4... | collective-permute-start | bytes 1376264 | tf_op jit(solution)/shard_map/ppermute | solution.py:131
  258.0 87.6 %collective-permute-start.13 = (bf16[14,128,128]{2,1,0:T(8,128)(2,1)S(1)}, bf16[14,128,128]{2,1,0:T(8,128)(2,1)S(1)}, u32[]{:S(2)}, u32[]{:S(2)}) collective-permute-start(bf16[14,128,128]{2,1,0:T(8,128)(2,1)S(1)} %multiply_convert_fusion), channel_id=1, source_target_pairs={{0,0},{1,128},{128,1},{129,129},{2,2},{3,130},{130,3},{131,131},{4... | collective-permute-start | bytes 1376264 | tf_op jit(solution)/shard_map/ppermute | solution.py:131
  336.4 9.2 %collective-permute-start.12 = (bf16[128,512]{1,0:T(8,128)(2,1)}, bf16[128,512]{1,0:T(8,128)(2,1)S(1)}, u32[]{:S(2)}, u32[]{:S(2)}) collective-permute-start(bf16[128,512]{1,0:T(8,128)(2,1)} %reduce-scatter.3.cloned.1.call-done), channel_id=1, source_target_pairs={{0,0},{1,128},{128,1},{129,129},{2,2},{3,130},{130,3},{131,131},{4... | collective-permute-start | bytes 393224 | tf_op jit(solution)/shard_map/ppermute | solution.py:131
Sparse Core Ops, SparseCore 0:
  21.4 93.3 all-gather.1
  155.1 101.7 reduce-scatter.4
  260.8 75.5 reduce-scatter.2

commit v2 on v1

v2 whole, which is shorter than its diff:
```python
import math

import jax
import jax.numpy as jnp
import numpy as np
from jax import lax
from jax.experimental import pallas as pl
from jax.experimental.pallas import tpu as pltpu
from jax.sharding import Mesh
from jax.sharding import PartitionSpec as P

AXES = ("xh", "xl", "z", "y", "core")
BS = 128
VMEM_LIMIT = 56 * 1024 * 1024

GATE_RUNS = [(d, r) for d in range(8) for r in (0, 1)]
UP_RUNS = [(d, r) for r in (0, 1) for d in range(8)]
EARLY_RUNS = 8


def tile(index):
    return pl.ds(pl.multiple_of(index * BS, BS), BS)


def start_copies(copies, block_refs, w_ref, sems):
    started = []
    for number, (which, start, size, target) in enumerate(copies):
        copy = pltpu.make_async_copy(
            block_refs[which].at[pl.ds(start, size)], w_ref.at[pl.ds(target, size)], sems.at[number]
        )
        copy.start()
        started.append(copy)
    return started


def over_runs(copies, started, count, run_first, run, body):
    early = EARLY_RUNS * run
    for piece, copy in zip(copies, started):
        if piece[3] < early:
            copy.wait()

    def visit(index, carry):
        first = run_first(index)

        @pl.when(first < count)
        def _():
            body(index, first)

        return carry

    lax.fori_loop(0, EARLY_RUNS, visit, 0)
    for piece, copy in zip(copies, started):
        if piece[3] >= early:
            copy.wait()
    lax.fori_loop(EARLY_RUNS, len(GATE_RUNS), visit, 0)


class Lists:
    def __init__(self, lists, place, table, matrix, capacity, run, nz):
        self.lists, self.place, self.table = lists, place, table
        self.rows, self.cols = 2 * matrix * capacity, (2 * matrix + 1) * capacity
        self.count = lists[4 * capacity + matrix]
        self.capacity, self.run, self.nz = capacity, run, nz

    def first(self, index):
        z = self.table[0, index]
        xl = self.place[0] ^ self.table[1, index]
        return (((self.place[1] ^ (z % 2)) * 2 + xl) * self.nz + z) * self.run

    def row(self, slot):
        return self.lists[self.rows + slot]

    def col(self, slot):
        return self.lists[self.cols + slot]


def table_of(runs):
    return jnp.asarray(np.asarray(runs, np.int32).T)


def forward_call(scalars, matrix, capacity, nz, x, blocks, copies, width, run):
    tok_rows = x.shape[0] // 2
    slots = len(GATE_RUNS) * run

    def kernel(lists, place, table, x_ref, *refs):
        block_refs = refs[: len(blocks)]
        own_ref, send_ref, acc_ref, w_ref, sems = refs[len(blocks) :]
        known = Lists(lists, place, table, matrix, capacity, run, nz)
        started = start_copies(copies, block_refs, w_ref, sems)
        acc_ref[...] = jnp.zeros_like(acc_ref)

        def body(index, first):
            for part in (range(0, 4), range(4, run)):
                products = []
                for u in part:
                    x = x_ref[:, tile(known.row(first + u))]
                    products.append(jnp.dot(x, w_ref[index * run + u], preferred_element_type=jnp.float32))
                for u, product in zip(part, products):
                    col = jnp.where(first + u < known.count, known.col(first + u), width // BS)
                    acc_ref[:, tile(col)] = acc_ref[:, tile(col)] + product

        over_runs(copies, started, known.count, known.first, run, body)
        half = place[2]
        own_ref[...] = acc_ref[tile(half), :width]
        send_ref[...] = acc_ref[tile(1 - half), :width]

    vmem = pl.BlockSpec(memory_space=pltpu.VMEM)
    out = jax.ShapeDtypeStruct((tok_rows, width), jnp.float32)
    return pl.pallas_call(
        kernel,
        name="forward",
        out_shape=(out, out),
        grid_spec=pltpu.PrefetchScalarGridSpec(
            num_scalar_prefetch=3,
            grid=(),
            in_specs=[vmem] + [pl.BlockSpec(memory_space=pl.ANY)] * len(blocks),
            out_specs=(vmem, vmem),
            scratch_shapes=[
                pltpu.VMEM((2 * tok_rows, width + BS), jnp.float32),
                pltpu.VMEM((slots, BS, BS), jnp.bfloat16),
                pltpu.SemaphoreType.DMA((len(copies),)),
            ],
        ),
        compiler_params=pltpu.CompilerParams(vmem_limit_bytes=VMEM_LIMIT),
        cost_estimate=pl.CostEstimate(
            flops=slots * 4 * tok_rows * BS * BS, transcendentals=0, bytes_accessed=8_000_000
        ),
    )(*scalars, x, *blocks)


def input_call(scalars, matrix, capacity, nz, own_g, mate_g, previous, blocks, copies, shape, run):
    tok_rows = own_g.shape[0]
    width = own_g.shape[1]
    features = shape[0] * shape[1] * shape[3]
    slots = len(GATE_RUNS) * run
    last = previous is not None
    previous = previous if last else ()

    def kernel(lists, place, table, own_g_ref, mate_g_ref, *refs):
        before = refs[: len(previous)]
        block_refs = refs[len(previous) : len(previous) + len(blocks)]
        own_ref, send_ref, acc_ref, g_ref, w_ref, sems = refs[len(previous) + len(blocks) :]
        known = Lists(lists, place, table, matrix, capacity, run, nz)
        started = start_copies(copies, block_refs, w_ref, sems)
        mine, other = tile(place[2]), tile(1 - place[2])
        if last:
            acc_ref[mine, :features] = before[0][...]
            acc_ref[other, :features] = before[1][...]
        else:
            acc_ref[...] = jnp.zeros_like(acc_ref)
        g_ref[mine, :] = own_g_ref[...]
        g_ref[other, :] = mate_g_ref[...]

        def body(index, first):
            for part in (range(0, 4), range(4, run)):
                products = []
                for u in part:
                    g = g_ref[:, tile(known.col(first + u))]
                    products.append(
                        lax.dot_general(
                            g,
                            w_ref[index * run + u],
                            (((1,), (1,)), ((), ())),
                            preferred_element_type=jnp.float32,
                        )
                    )
                for u, product in zip(part, products):
                    row = jnp.where(first + u < known.count, known.row(first + u), features // BS)
                    acc_ref[:, tile(row)] = acc_ref[:, tile(row)] + product

        over_runs(copies, started, known.count, known.first, run, body)
        if last:
            step = shape[3]
            for high in range(shape[0]):
                for y in range(shape[1]):
                    cut = pl.ds((y * shape[0] + high) * step, step)
                    own_ref[high, y] = acc_ref[mine, cut].astype(own_ref.dtype)
                    send_ref[high, y] = acc_ref[other, cut].astype(send_ref.dtype)
        else:
            own_ref[...] = acc_ref[mine, :features]
            send_ref[...] = acc_ref[other, :features]

    vmem = pl.BlockSpec(memory_space=pltpu.VMEM)
    out = (
        jax.ShapeDtypeStruct(shape, jnp.bfloat16)
        if last
        else jax.ShapeDtypeStruct((tok_rows, features), jnp.float32)
    )
    return pl.pallas_call(
        kernel,
        name="input_grad",
        out_shape=(out, out),
        grid_spec=pltpu.PrefetchScalarGridSpec(
            num_scalar_prefetch=3,
            grid=(),
            in_specs=[vmem] * (2 + len(previous)) + [pl.BlockSpec(memory_space=pl.ANY)] * len(blocks),
            out_specs=(vmem, vmem),
            scratch_shapes=[
                pltpu.VMEM((2 * tok_rows, features + BS), jnp.float32),
                pltpu.VMEM((2 * tok_rows, width), jnp.bfloat16),
                pltpu.VMEM((slots, BS, BS), jnp.bfloat16),
                pltpu.SemaphoreType.DMA((len(copies),)),
            ],
        ),
        compiler_params=pltpu.CompilerParams(vmem_limit_bytes=VMEM_LIMIT),
        cost_estimate=pl.CostEstimate(
            flops=slots * 4 * tok_rows * BS * BS, transcendentals=0, bytes_accessed=12_000_000
        ),
    )(*scalars, own_g, mate_g, *previous, *blocks)


def weight_call(scalars, matrix, capacity, nz, own_g, mate_g, xt, first_run, sizes, run):
    tok_rows = own_g.shape[0]
    width = own_g.shape[1]

    def kernel(lists, place, table, own_g_ref, mate_g_ref, xt_ref, *refs):
        outs, g_ref = refs[:-1], refs[-1]
        known = Lists(lists, place, table, matrix, capacity, run, nz)
        g_ref[tile(place[2]), :] = own_g_ref[...]
        g_ref[tile(1 - place[2]), :] = mate_g_ref[...]
        base = first_run
        for out_ref, runs in zip(outs, sizes):

            def visit(index, carry, out_ref=out_ref, base=base):
                first = known.first(base + index)

                @pl.when(first < known.count)
                def _():
                    for u in range(run):
                        term = jnp.dot(
                            xt_ref[tile(known.row(first + u)), :],
                            g_ref[:, tile(known.col(first + u))],
                            preferred_element_type=jnp.float32,
                        )
                        term = jnp.where(first + u < known.count, term, 0.0)
                        out_ref[index * run + u] = term.astype(out_ref.dtype)

                @pl.when(first >= known.count)
                def _():
                    for u in range(run):
                        out_ref[index * run + u] = jnp.zeros((BS, BS), out_ref.dtype)

                return carry

            lax.fori_loop(0, runs, visit, 0)
            base = base + runs

    vmem = pl.BlockSpec(memory_space=pltpu.VMEM)
    return pl.pallas_call(
        kernel,
        name="weight_grad",
        out_shape=tuple(jax.ShapeDtypeStruct((runs * run, BS, BS), jnp.bfloat16) for runs in sizes),
        grid_spec=pltpu.PrefetchScalarGridSpec(
            num_scalar_prefetch=3,
            grid=(),
            in_specs=[vmem] * 3,
            out_specs=tuple(vmem for _ in sizes),
            scratch_shapes=[pltpu.VMEM((2 * tok_rows, width), jnp.bfloat16)],
        ),
        compiler_params=pltpu.CompilerParams(vmem_limit_bytes=VMEM_LIMIT),
        cost_estimate=pl.CostEstimate(
            flops=sum(sizes) * run * 4 * tok_rows * BS * BS,
            transcendentals=0,
            bytes_accessed=4_000_000 + sum(sizes) * run * 32768,
        ),
    )(*scalars, own_g, mate_g, xt)


def add(*parts):
    total = parts[0].astype(jnp.float32)
    for part in parts[1:]:
        total = total + part.astype(jnp.float32)
    return total.astype(jnp.bfloat16)


def rounds(*values):
    return lax.optimization_barrier(values)


def on_device(
    tokens,
    hidden_grad,
    gate_blocks,
    up_blocks,
    gate_rows,
    gate_cols,
    gate_count,
    up_rows,
    up_cols,
    up_count,
):
    nz, ny = lax.axis_size("z"), lax.axis_size("y")
    side, xl, zid, yid, core = (lax.axis_index(name) for name in AXES)
    half = core ^ (zid % 2)
    home = side == core
    tok_rows = tokens.shape[0]
    run = gate_blocks.shape[1]
    capacity = gate_rows.shape[1]
    width = hidden_grad.shape[1]
    row_blocks = 2 * ny * tokens.shape[1] // BS

    moves = []
    for xh in range(2):
        for z in range(nz):
            for c in range(2):
                moves.append((((c ^ (z % 2)) * nz + z) * 2 + xh, (xh * nz + z) * 2 + c))

    def swap_in(value):
        return lax.ppermute(value, ("xh", "z", "core"), moves)

    def swap_out(value):
        return lax.ppermute(value, ("xh", "z", "core"), [(b, a) for a, b in moves])

    def mate(value):
        return lax.ppermute(value, "core", [(0, 1), (1, 0)])

    def across(value):
        return lax.ppermute(value, "xl", [(0, 1), (1, 0)])

    up_own = swap_in(up_blocks[0])
    up_all = lax.all_gather(up_own, "z", axis=0, tiled=True)
    gate_own = swap_in(gate_blocks[0])
    gate_both = jnp.concatenate([gate_own, across(gate_own)], axis=0)
    packed = jnp.concatenate(
        [gate_rows[0], gate_cols[0], up_rows[0], up_cols[0], gate_count, up_count]
    )
    packed = jnp.where(home, packed, mate(packed))
    other = lax.ppermute(tokens, "xh", [(0, 1), (1, 0)])
    pair = jnp.concatenate(
        [jnp.where(side == 0, tokens, other), jnp.where(side == 0, other, tokens)], axis=0
    )
    from_y = [pair] + [
        lax.ppermute(pair, "y", [(i, (i + s) % ny) for i in range(ny)]) for s in range(1, ny)
    ]
    from_y = jnp.stack(from_y)
    from_y = jnp.stack(
        [lax.dynamic_index_in_dim(from_y, (yid - i) % ny, 0, keepdims=False) for i in range(ny)]
    )
    from_mate = mate(from_y)
    upstream = swap_in(hidden_grad)
    gate_both, up_all, from_mate, upstream, packed = rounds(
        gate_both, up_all, from_mate, upstream, packed
    )
    gate_all = lax.all_gather(gate_both, "z", axis=0, tiled=True)
    up_beside = across(up_all)
    by_core = jnp.stack(
        [jnp.where(core == 0, from_y, from_mate), jnp.where(core == 0, from_mate, from_y)], axis=1
    )
    x = by_core.transpose(2, 0, 1, 3).reshape(2 * tok_rows, row_blocks * BS)
    xt = x.T
    here = jnp.stack([xl, core, half]).astype(jnp.int32)
    gate_scalars = (packed, here, table_of(GATE_RUNS))
    up_scalars = (packed, here, table_of(UP_RUNS))
    part = len(UP_RUNS) // 2 * run
    up_copies = [(0, 0, part, 0), (1, 0, part, part)]

    gate_parts, gate_copies = (gate_all,), [(0, 0, part, 0), (0, part, part, part)]
    up_parts = (up_all, up_beside)

    up_kept, up_sent = forward_call(up_scalars, 1, capacity, nz, x, up_parts, up_copies, width, run)
    up_sent = mate(up_sent)
    gate_kept, gate_sent = forward_call(
        gate_scalars, 0, capacity, nz, x, gate_parts, gate_copies, width, run
    )
    up = up_kept + up_sent
    gate = gate_kept + mate(gate_sent)
    upstream = upstream.astype(jnp.float32)
    sigma = jax.nn.sigmoid(gate)
    activated = gate * sigma
    slope = sigma * (1.0 + gate * (1.0 - sigma))
    gate_grad = (upstream * up * slope).astype(jnp.bfloat16)
    up_grad = (upstream * activated).astype(jnp.bfloat16)
    hidden = (activated * up).astype(jnp.bfloat16)
    gate_mate = mate(gate_grad)
    up_mate = mate(up_grad)

    (gate_terms,) = weight_call(
        gate_scalars, 0, capacity, nz, gate_grad, gate_mate, xt, 0, (len(GATE_RUNS),), run
    )
    gate_sum = lax.psum_scatter(gate_terms, "z", scatter_dimension=0, tiled=True)
    up_mate, gate_terms, hidden = rounds(up_mate, gate_terms, hidden)
    half_runs = len(UP_RUNS) // 2
    up_terms, up_sent = weight_call(
        up_scalars, 1, capacity, nz, up_grad, up_mate, xt, 0, (half_runs, half_runs), run
    )
    up_sent, up_terms, up_mate = rounds(up_sent, up_terms, up_mate)
    up_got = across(up_sent)

    shape = (2, ny, tok_rows, tokens.shape[1])
    shares = input_call(
        up_scalars, 1, capacity, nz, up_grad, up_mate, None, up_parts, up_copies, shape, run
    )
    own, send = input_call(
        gate_scalars, 0, capacity, nz, gate_grad, gate_mate, shares, gate_parts, gate_copies, shape, run
    )
    share = add(own, mate(send))
    kept = lax.dynamic_index_in_dim(share, side, 0, keepdims=False)
    given = lax.dynamic_index_in_dim(share, 1 - side, 0, keepdims=False)
    up_got, given = rounds(up_got, given)
    up_terms = add(up_terms, up_got)
    up_sum = lax.psum_scatter(up_terms, "z", scatter_dimension=0, tiled=True)
    share = add(kept, lax.ppermute(given, "xh", [(0, 1), (1, 0)]))
    total = lax.dynamic_index_in_dim(share, yid, 0, keepdims=False).astype(jnp.float32)
    for step in range(1, ny):
        term = lax.dynamic_index_in_dim(share, (yid + step) % ny, 0, keepdims=False)
        term = lax.ppermute(term, "y", [(i, (i + step) % ny) for i in range(ny)])
        total = total + term.astype(jnp.float32)
    input_grad = swap_out(total.astype(jnp.bfloat16))
    hidden = swap_out(hidden)

    scale = 1.0 / math.sqrt(tok_rows * 4 * nz)
    gate_total = gate_sum[:run].astype(jnp.float32) + across(gate_sum[run:]).astype(jnp.float32)
    gate_out = swap_out((gate_total * scale).astype(jnp.bfloat16))
    up_sum, input_grad, hidden, gate_out = rounds(up_sum, input_grad, hidden, gate_out)
    up_out = swap_out((up_sum.astype(jnp.float32) * scale).astype(jnp.bfloat16))
    return hidden, input_grad, gate_out[None], up_out[None]


def solution(mesh):
    shape = mesh.devices.shape
    fine = Mesh(mesh.devices.reshape(2, 2, shape[0] // 4, shape[1] // 2, 2), AXES)
    seq, hid = ("xh", "xl", "z"), ("y", "core")
    placed = (
        P(seq, hid),
        P(seq, hid),
        P(hid, seq, None, None),
        P(hid, seq, None, None),
        P(hid, None),
        P(hid, None),
        P(hid),
        P(hid, None),
        P(hid, None),
        P(hid),
    )
    return jax.shard_map(
        on_device,
        mesh=fine,
        in_specs=placed,
        out_specs=(P(seq, hid), P(seq, hid), P(hid, seq, None, None), P(hid, seq, None, None)),
        check_vma=False,
    )
```

time: 353 us -> 255 us (0.72)
  waiting for transfers between devices: 225 us -> 108 us
  Pallas kernels: 20.3 us -> 38.6 us
  starting transfers between devices: 72.8 us -> 64.5 us
    reduce_scatter x2, waiting for transfers between devices: 133 us -> 0.37 us  [the longest x1 0.35 us: on_device(): up_sum = lax.psum_scatter(up_terms, 'z', scatter_dimension=0, tiled=True)]
    ppermute x5 -> x15, waiting for transfers between devices: 13.3 us -> 78 us  [the longest x4 57 us: across(): return lax.ppermute(value, 'xl', [(0, 1), (1, 0)])]
    all_gather x1 -> x2, waiting for transfers between devices: 56.7 us -> 4.12 us  [the longest x1 4.11 us: on_device(): gate_all = lax.all_gather(gate_both, 'z', axis=0, tiled=True)]
    pallas_call x3 -> x6, Pallas kernels: 20.3 us -> 38.6 us  [the longest x2 14.1 us: input_call(): pl.pallas_call(kernel, name='input_grad', out_shape=(out, out), grid_spec...]
    ppermute x5 -> x7, starting transfers between devices: 20 us -> 4.64 us  [mate(): return lax.ppermute(value, 'core', [(0, 1), (1, 0)])]
    ppermute x5 -> x15, starting transfers between devices: 48.7 us -> 54.6 us  [the longest x4 23 us: swap_out(): return lax.ppermute(value, ('xh', 'z', 'core'), [(b, a) for a, b in moves])]
    ppermute x1, waiting for transfers between devices: 0.96 us -> 6.7 us  [on_device(): other = lax.ppermute(tokens, 'xh', [(0, 1), (1, 0)])]
    convert_element_type x2 -> x7, other arithmetic: 3.58 us -> 7.87 us  [the longest x3 4.06 us: add(): return total.astype(jnp.bfloat16)]
  transfers between devices with their start and end apart: 17 -> 30, of which waited for: 13 -> 19; matrix products, arithmetic and copies ran while one was open for 4% -> 7% of each run, Pallas kernels for 2% -> 13%
where the time goes in v2:
time: 255 us; the launch traced here: 254 us
  waiting for transfers between devices  108 us (42%)
  starting transfers between devices  64.5 us (25%)
  Pallas kernels  38.6 us (15%)
  between operations  15.5 us (6%)
  other arithmetic  13.8 us (5%)
  local copies, waits for them, and re-layouts  13.1 us (5%)
    ppermute x4, waiting for transfers between devices, across(): return lax.ppermute(value, 'xl', [(0, 1), (1, 0)])  57 us
    ppermute x4, starting transfers between devices, swap_out(): return lax.ppermute(value, ('xh', 'z', 'core'), [(b, a) for a, b in moves])  23 us
    pallas_call x2, Pallas kernels, input_call(): pl.pallas_call(kernel, name='input_grad', out_shape=(out, out), grid_spec...  14.1 us
    ppermute x3, starting transfers between devices, swap_in(): return lax.ppermute(value, ('xh', 'z', 'core'), moves)  13.1 us
    pallas_call x2, Pallas kernels, forward_call(): pl.pallas_call(kernel, name='forward', out_shape=(out, out), grid_spec=pl...  12.5 us
    pallas_call x2, Pallas kernels, weight_call(): pl.pallas_call(kernel, name='weight_grad', out_shape=tuple((jax.ShapeDtyp...  12 us
    ppermute x3, waiting for transfers between devices, on_device(): lax.ppermute(pair, 'y', [(i, (i + s) % ny) for i in range(ny)])  9.99 us
    ppermute x3, starting transfers between devices, on_device(): term = lax.ppermute(term, 'y', [(i, (i + step) % ny) for i in range(ny)])  8.9 us
  transfers between devices with their start and end apart: 30, of which 19 were waited for; matrix products, arithmetic and copies ran while one was open for 7% of the time, Pallas kernels for 13%

profile of v2, /device:TPU:1, one launch (start us, length us, event | category | flops | bytes accessed | tf_op | source)
XLA Modules:
  0.0 253.6 jit_solution(3378402244215802950)
XLA Ops:
  7.2 6.0 %collective-permute-start.2 = (bf16[7,128,128]{2,1,0:T(8,128)(2,1)}, bf16[7,128,128]{2,1,0:T(8,128)(2,1)S(1)}, u32[]{:S(2)}, u32[]{:S(2)}) collective-permute-start(bf16[7,128,128]{2,1,0:T(8,128)(2,1)} %bitcast.51), channel_id=1, source_target_pairs={{0,0},{128,1},{136,8},{8,9},{16,16},{144,17},{152,24},{24,25},{32,... | collective-permute-start | bytes 688136 | tf_op jit(solution)/shard_map/ppermute | solution.py:309
  13.3 3.9 %collective-permute-done.2 = bf16[7,128,128]{2,1,0:T(8,128)(2,1)S(1)} collective-permute-done((bf16[7,128,128]{2,1,0:T(8,128)(2,1)}, bf16[7,128,128]{2,1,0:T(8,128)(2,1)S(1)}, u32[]{:S(2)}, u32[]{:S(2)}) %collective-permute-start.2) | collective-permute-done | bytes 229408 | tf_op jit(solution)/shard_map/ppermute | solution.py:309
  17.2 0.7 copy-done.9
  18.0 6.7 %collective-permute-done.3 = bf16[128,512]{1,0:T(8,128)(2,1)S(1)} collective-permute-done((bf16[128,512]{1,0:T(8,128)(2,1)}, bf16[128,512]{1,0:T(8,128)(2,1)S(1)}, u32[]{:S(2)}, u32[]{:S(2)}) %collective-permute-start.3) | collective-permute-done | bytes 131104 | tf_op jit(solution)/shard_map/ppermute | solution.py:328
  24.7 0.9 broadcast_select_fusion.1
  25.7 1.4 collective-permute-start.4
  27.1 2.6 %collective-permute-start.5 = (bf16[256,512]{1,0:T(8,128)(2,1)S(1)}, bf16[256,512]{1,0:T(8,128)(2,1)S(1)}, u32[]{:S(2)}, u32[]{:S(2)}) collective-permute-start(bf16[256,512]{1,0:T(8,128)(2,1)S(1)} %get-tuple-element.69), channel_id=1, source_target_pairs={{0,4},{2,6},{4,0},{6,2},{1,5},{3,7},{5,1},{7,3},{8,12},{10,14},{12... | collective-permute-start | bytes 786440 | tf_op jit(solution)/shard_map/ppermute | solution.py:333
  29.7 1.1 collective-permute-start.6
  30.8 3.3 %collective-permute-done.4 = bf16[256,512]{1,0:T(8,128)(2,1)S(1)} collective-permute-done((bf16[256,512]{1,0:T(8,128)(2,1)S(1)}, bf16[256,512]{1,0:T(8,128)(2,1)S(1)}, u32[]{:S(2)}, u32[]{:S(2)}) %collective-permute-start.4) | collective-permute-done | bytes 262176 | tf_op jit(solution)/shard_map/ppermute | solution.py:333
  34.0 6.7 %collective-permute-done.5 = bf16[256,512]{1,0:T(8,128)(2,1)S(1)} collective-permute-done((bf16[256,512]{1,0:T(8,128)(2,1)S(1)}, bf16[256,512]{1,0:T(8,128)(2,1)S(1)}, u32[]{:S(2)}, u32[]{:S(2)}) %collective-permute-start.5) | collective-permute-done | bytes 262176 | tf_op jit(solution)/shard_map/ppermute | solution.py:333
  41.2 1.9 collective-permute-start.7
  43.1 1.9 collective-permute-start
  45.0 5.1 %collective-permute-start.8 = (bf16[128,1792]{1,0:T(8,128)(2,1)}, bf16[128,1792]{1,0:T(8,128)(2,1)}, u32[]{:S(2)}, u32[]{:S(2)}) collective-permute-start(bf16[128,1792]{1,0:T(8,128)(2,1)} %param.13), channel_id=1, source_target_pairs={{0,0},{128,1},{136,8},{8,9},{16,16},{144,17},{152,24},{24,25},{32,... | collective-permute-start | bytes 1376264 | tf_op jit(solution)/shard_map/ppermute | solution.py:309
  50.2 2.5 collective-permute-done
  52.6 3.2 %collective-permute-start.1 = (bf16[7,128,128]{2,1,0:T(8,128)(2,1)S(1)}, bf16[7,128,128]{2,1,0:T(8,128)(2,1)}, u32[]{:S(2)}, u32[]{:S(2)}) collective-permute-start(bf16[7,128,128]{2,1,0:T(8,128)(2,1)S(1)} %collective-permute-done), channel_id=1, source_target_pairs={{0,64},{64,0},{1,65},{65,1},{2,66},{66,2},{3,67},{67,3},{4,68},{68... | collective-permute-start | bytes 688136 | tf_op jit(solution)/shard_map/ppermute | solution.py:318
  57.3 1.1 collective-permute-done.9
  58.5 0.6 broadcast_select_fusion.2.lists
  59.1 3.1 %collective-permute-done.1 = bf16[7,128,128]{2,1,0:T(8,128)(2,1)} collective-permute-done((bf16[7,128,128]{2,1,0:T(8,128)(2,1)S(1)}, bf16[7,128,128]{2,1,0:T(8,128)(2,1)}, u32[]{:S(2)}, u32[]{:S(2)}) %collective-permute-start.1) | collective-permute-done | bytes 229408 | tf_op jit(solution)/shard_map/ppermute | solution.py:318
  62.2 1.7 pad_maximum_fusion.2
  64.1 0.6 collective-permute-start.12
  64.6 0.6 pad_add_fusion.place
  65.4 1.5 maximum_bitcast_fusion
  67.0 2.8 %copy.19 = bf16[256,4,2,512]{0,3,2,1:T(8,128)(2,1)S(1)} copy(bf16[256,4,2,512]{3,0,1,2:T(8,128)(2,1)} %maximum_bitcast_fusion) | data formatting | bytes 4194304 | tf_op jit(solution)/shard_map/transpose | solution.py:349
  69.8 3.0 %copy.20.x_ref = bf16[256,4096]{1,0:T(8,128)(2,1)} copy(bf16[256,4096]{0,1:T(8,128)(2,1)S(1)} %bitcast.39) | data formatting | bytes 4194304 | tf_op jit(solution)/shard_map/reshape | solution.py:349
  72.8 31.9 %collective-permute-done.12.refs_1_ = bf16[56,128,128]{2,1,0:T(8,128)(2,1)} collective-permute-done((bf16[56,128,128]{2,1,0:T(8,128)(2,1)}, bf16[56,128,128]{2,1,0:T(8,128)(2,1)}, u32[]{:S(2)}, u32[]{:S(2)}) %collective-permute-start.12) | collective-permute-done | bytes 1835040 | tf_op jit(solution)/shard_map/ppermute | solution.py:318
  104.7 6.1 %forward.3 = (f32[128,1792]{1,0:T(8,128)}, f32[128,1792]{1,0:T(8,128)}) custom-call(s32[898]{0:T(1024)} %broadcast_select_fusion.2.lists, s32[3]{0:T(128)} %pad_add_fusion.place, s32[2,16]{1,0:T(2,128)} %constant.111.clone.table, bf16[256,4096]{1,0:T(8,128)(2,1)} %copy.20.x_ref, bf16[56,128,128]{2,1,0:T(8,128)(2,1)} %all-gather.3.cloned.1.call-done.refs_0_, ...), custom_call_target="tpu_custom_call" | custom-call | flops 939524096 | bytes 8000000 | tf_op jit(solution)/shard_map/forward/pallas_call | solution.py:109
  110.9 4.1 %all-gather.5.cloned.1.call-done.refs_0_.refs_2_ = bf16[112,128,128]{2,1,0:T(8,128)(2,1)} async-done(((bf16[14,128,128]{2,1,0:T(8,128)(2,1)}), bf16[112,128,128]{2,1,0:T(8,128)(2,1)}) %all-gather.5.cloned.1.call-update) | async-done | bytes 3670032 | tf_op jit(solution)/shard_map/all_gather | solution.py:344
  115.0 6.4 %forward.2 = (f32[128,1792]{1,0:T(8,128)}, f32[128,1792]{1,0:T(8,128)}) custom-call(s32[898]{0:T(1024)} %broadcast_select_fusion.2.lists, s32[3]{0:T(128)} %pad_add_fusion.place, s32[2,16]{1,0:T(2,128)} %constant.110.clone.table, bf16[256,4096]{1,0:T(8,128)(2,1)} %copy.20.x_ref, bf16[112,128,128]{2,1,0:T(8,128)(2,1)} %all-gather.5.cloned.1.call-done.refs_0_.refs_2_), custom_call_target="tpu_custom_call" | custom-call | flops 939524096 | bytes 8000000 | tf_op jit(solution)/shard_map/forward/pallas_call | solution.py:109
  121.4 0.8 collective-permute-start.10
  122.2 2.3 collective-permute-done.10
  124.5 2.7 %multiply_convert_fusion = (bf16[128,1792]{1,0:T(8,128)(2,1)}, bf16[128,1792]{1,0:T(8,128)(2,1)S(1)}, bf16[128,1792]{1,0:T(8,128)(2,1)S(1)}) fusion(f32[128,1792]{1,0:T(8,128)S(1)} %copy-done.6, f32[128,1792]{1,0:T(8,128)S(1)} %collective-permute-done.13, f32[128,1792]{1,0:T(8,128)} %get-tuple-element.34, f32[128,1792]{1,0:T(8,128)S(1)} %collective-permute-done.10, ...), kind=kLoop, calls=%fused_computation.14 | loop fusion | flops 4128768 | bytes 5505024 | tf_op jit(solution)/shard_map/convert_element_type | solution.py:373
  127.6 1.4 collective-permute-done.14.mate_g_ref
  129.0 0.8 copy-done.3
  129.8 6.1 %weight_grad.2 = bf16[112,128,128]{2,1,0:T(8,128)(2,1)} custom-call(s32[898]{0:T(1024)} %broadcast_select_fusion.2.lists, s32[3]{0:T(128)} %pad_add_fusion.place, s32[2,16]{1,0:T(2,128)} %constant.110.clone.table, bf16[128,1792]{1,0:T(8,128)(2,1)} %copy-done.1, bf16[128,1792]{1,0:T(8,128)(2,1)} %copy-done.3, bf16[4096,256]{1,0:T(8,128)(2,1)} %bitcast.40), custom_call_target="tpu_custom_call" | custom-call | flops 939524096 | bytes 7670016 | tf_op jit(solution)/shard_map/weight_grad/pallas_call | solution.py:249
  136.0 0.6 collective-permute-start.11
  136.6 1.4 collective-permute-done.11.mate_g_ref
  138.1 0.8 copy-done.7
  138.9 5.9 %weight_grad.3 = (bf16[56,128,128]{2,1,0:T(8,128)(2,1)}, bf16[56,128,128]{2,1,0:T(8,128)(2,1)}) custom-call(s32[898]{0:T(1024)} %broadcast_select_fusion.2.lists, s32[3]{0:T(128)} %pad_add_fusion.place, s32[2,16]{1,0:T(2,128)} %constant.111.clone.table, bf16[128,1792]{1,0:T(8,128)(2,1)} %copy-done.2, bf16[128,1792]{1,0:T(8,128)(2,1)} %copy-done.7, ...), custom_call_target="tpu_custom_call" | custom-call | flops 939524096 | bytes 7670016 | tf_op jit(solution)/shard_map/weight_grad/pallas_call | solution.py:249
  144.7 1.2 collective-permute-start.15
  145.9 6.6 %input_grad.2 = (f32[128,4096]{1,0:T(8,128)}, f32[128,4096]{1,0:T(8,128)}) custom-call(s32[898]{0:T(1024)} %broadcast_select_fusion.2.lists, s32[3]{0:T(128)} %pad_add_fusion.place, s32[2,16]{1,0:T(2,128)} %constant.111.clone.table, bf16[128,1792]{1,0:T(8,128)(2,1)} %copy-done.2, bf16[128,1792]{1,0:T(8,128)(2,1)} %copy-done.7, ...), custom_call_target="tpu_custom_call" | custom-call | flops 939524096 | bytes 12000000 | tf_op jit(solution)/shard_map/input_grad/pallas_call | solution.py:189
  152.5 7.5 %input_grad.3 = (bf16[2,4,128,512]{3,2,1,0:T(8,128)(2,1)}, bf16[2,4,128,512]{3,2,1,0:T(8,128)(2,1)}) custom-call(s32[898]{0:T(1024)} %broadcast_select_fusion.2.lists, s32[3]{0:T(128)} %pad_add_fusion.place, s32[2,16]{1,0:T(2,128)} %constant.110.clone.table, bf16[128,1792]{1,0:T(8,128)(2,1)} %copy-done.1, bf16[128,1792]{1,0:T(8,128)(2,1)} %copy-done.3, ...), custom_call_target="tpu_custom_call" | custom-call | flops 939524096 | bytes 12000000 | tf_op jit(solution)/shard_map/input_grad/pallas_call | solution.py:189
  160.0 0.8 collective-permute-start.16
  160.8 2.5 collective-permute-done.16
  163.3 1.0 copy-done.5
  164.3 2.0 add_convert_fusion.1
  166.4 19.9 %collective-permute-done.15 = bf16[56,128,128]{2,1,0:T(8,128)(2,1)S(1)} collective-permute-done((bf16[56,128,128]{2,1,0:T(8,128)(2,1)}, bf16[56,128,128]{2,1,0:T(8,128)(2,1)S(1)}, u32[]{:S(2)}, u32[]{:S(2)}) %collective-permute-start.15) | collective-permute-done | bytes 1835040 | tf_op jit(solution)/shard_map/ppermute | solution.py:318
  186.3 1.9 add_convert_fusion
  188.2 4.1 %collective-permute-start.17 = (bf16[4,128,512]{2,1,0:T(8,128)(2,1)S(1)}, bf16[4,128,512]{2,1,0:T(8,128)(2,1)S(1)}, u32[]{:S(2)}, u32[]{:S(2)}) collective-permute-start(bf16[4,128,512]{2,1,0:T(8,128)(2,1)S(1)} %dynamic-slice_bitcast_fusion), channel_id=1, source_target_pairs={{0,128},{128,0},{1,129},{129,1},{2,130},{130,2},{3,131},{131,3},{4... | collective-permute-start | bytes 1572872 | tf_op jit(solution)/shard_map/ppermute | solution.py:402
  192.4 3.0 %collective-permute-start.22 = (bf16[128,1792]{1,0:T(8,128)(2,1)}, bf16[128,1792]{1,0:T(8,128)(2,1)S(1)}, u32[]{:S(2)}, u32[]{:S(2)}) collective-permute-start(bf16[128,1792]{1,0:T(8,128)(2,1)} %get-tuple-element.51), channel_id=1, source_target_pairs={{0,0},{1,128},{8,136},{9,8},{16,16},{17,144},{24,152},{25,24},{32,... | collective-permute-start | bytes 1376264 | tf_op jit(solution)/shard_map/ppermute | solution.py:312
  195.4 1.0 slice.9
  196.8 6.7 %collective-permute-done.17 = bf16[4,128,512]{2,1,0:T(8,128)(2,1)S(1)} collective-permute-done((bf16[4,128,512]{2,1,0:T(8,128)(2,1)S(1)}, bf16[4,128,512]{2,1,0:T(8,128)(2,1)S(1)}, u32[]{:S(2)}, u32[]{:S(2)}) %collective-permute-start.17) | collective-permute-done | bytes 524320 | tf_op jit(solution)/shard_map/ppermute | solution.py:402
  203.7 6.4 %collective-permute-start.18 = (bf16[128,512]{1,0:T(8,128)(2,1)S(1)}, bf16[128,512]{1,0:T(8,128)(2,1)S(1)}, u32[]{:S(2)}, u32[]{:S(2)}) collective-permute-start(bf16[128,512]{1,0:T(8,128)(2,1)S(1)} %get-tuple-element.65), channel_id=1, source_target_pairs={{0,2},{2,4},{4,6},{6,0},{1,3},{3,5},{5,7},{7,1},{8,10},{10,12},{12... | collective-permute-start | bytes 393224 | tf_op jit(solution)/shard_map/ppermute | solution.py:406
  210.1 2.5 collective-permute-start.20
  212.6 2.0 collective-permute-done.23
  214.7 7.4 %collective-permute-start.24 = (bf16[7,128,128]{2,1,0:T(8,128)(2,1)S(1)}, bf16[7,128,128]{2,1,0:T(8,128)(2,1)S(1)}, u32[]{:S(2)}, u32[]{:S(2)}) collective-permute-start(bf16[7,128,128]{2,1,0:T(8,128)(2,1)S(1)} %multiply_convert_fusion.2), channel_id=1, source_target_pairs={{0,0},{1,128},{8,136},{9,8},{16,16},{17,144},{24,152},{25,24},{32,... | collective-permute-start | bytes 688136 | tf_op jit(solution)/shard_map/ppermute | solution.py:312
  222.3 3.6 %collective-permute-start.21 = (bf16[128,512]{1,0:T(8,128)(2,1)S(1)}, bf16[128,512]{1,0:T(8,128)(2,1)S(1)}, u32[]{:S(2)}, u32[]{:S(2)}) collective-permute-start(bf16[128,512]{1,0:T(8,128)(2,1)S(1)} %fusion.7), channel_id=1, source_target_pairs={{0,0},{1,128},{8,136},{9,8},{16,16},{17,144},{24,152},{25,24},{32,... | collective-permute-start | bytes 393224 | tf_op jit(solution)/shard_map/ppermute | solution.py:312
  225.8 4.2 %collective-permute-done.21 = bf16[128,512]{1,0:T(8,128)(2,1)S(1)} collective-permute-done((bf16[128,512]{1,0:T(8,128)(2,1)S(1)}, bf16[128,512]{1,0:T(8,128)(2,1)S(1)}, u32[]{:S(2)}, u32[]{:S(2)}) %collective-permute-start.21) | collective-permute-done | bytes 131104 | tf_op jit(solution)/shard_map/ppermute | solution.py:312
  230.4 1.0 multiply_convert_fusion.1
  231.4 9.1 %collective-permute-start.25 = (bf16[7,128,128]{2,1,0:T(8,128)(2,1)S(1)}, bf16[7,128,128]{2,1,0:T(8,128)(2,1)S(1)}, u32[]{:S(2)}, u32[]{:S(2)}) collective-permute-start(bf16[7,128,128]{2,1,0:T(8,128)(2,1)S(1)} %multiply_convert_fusion.1), channel_id=1, source_target_pairs={{0,0},{1,128},{8,136},{9,8},{16,16},{17,144},{24,152},{25,24},{32,... | collective-permute-start | bytes 688136 | tf_op jit(solution)/shard_map/ppermute | solution.py:312
  240.5 3.7 %collective-permute-done.25 = bf16[7,128,128]{2,1,0:T(8,128)(2,1)S(1)} collective-permute-done((bf16[7,128,128]{2,1,0:T(8,128)(2,1)S(1)}, bf16[7,128,128]{2,1,0:T(8,128)(2,1)S(1)}, u32[]{:S(2)}, u32[]{:S(2)}) %collective-permute-start.25) | collective-permute-done | bytes 229408 | tf_op jit(solution)/shard_map/ppermute | solution.py:312
  244.2 0.8 copy.28
  245.0 0.7 copy.29
  245.6 0.7 copy.30
  246.3 0.7 copy.31
  (63 shorter events, 2.7 us)
Async XLA Ops:
  7.2 56.8 %all-gather.3.cloned.1.call-start = ((), (), s32[]{:S(2)}) async-start(), calls=%async_computation.2 | async-start | bytes 2064384 | tf_op jit(solution)/shard_map/all_gather | solution.py:321
  7.2 9.9 %collective-permute-start.2 = (bf16[7,128,128]{2,1,0:T(8,128)(2,1)}, bf16[7,128,128]{2,1,0:T(8,128)(2,1)S(1)}, u32[]{:S(2)}, u32[]{:S(2)}) collective-permute-start(bf16[7,128,128]{2,1,0:T(8,128)(2,1)} %bitcast.51), channel_id=1, source_target_pairs={{0,0},{128,1},{136,8},{8,9},{16,16},{144,17},{152,24},{24,25},{32,... | collective-permute-start | bytes 688136 | tf_op jit(solution)/shard_map/ppermute | solution.py:309
  17.2 0.7 copy-start.9
  17.9 97.2 %all-gather.5.cloned.1.call-start = ((), (), s32[]{:S(2)}) async-start(), calls=%async_computation.3 | async-start | bytes 4128768 | tf_op jit(solution)/shard_map/all_gather | solution.py:344
  17.9 6.8 %collective-permute-start.3 = (bf16[128,512]{1,0:T(8,128)(2,1)}, bf16[128,512]{1,0:T(8,128)(2,1)S(1)}, u32[]{:S(2)}, u32[]{:S(2)}) collective-permute-start(bf16[128,512]{1,0:T(8,128)(2,1)} %param.12), channel_id=1, source_target_pairs={{0,128},{128,0},{1,129},{129,1},{2,130},{130,2},{3,131},{131,3},{4... | collective-permute-start | bytes 393224 | tf_op jit(solution)/shard_map/ppermute | solution.py:328
  25.7 8.3 %collective-permute-start.4 = (bf16[256,512]{1,0:T(8,128)(2,1)S(1)}, bf16[256,512]{1,0:T(8,128)(2,1)S(1)}, u32[]{:S(2)}, u32[]{:S(2)}) collective-permute-start(bf16[256,512]{1,0:T(8,128)(2,1)S(1)} %get-tuple-element.69), channel_id=1, source_target_pairs={{0,2},{2,4},{4,6},{6,0},{1,3},{3,5},{5,7},{7,1},{8,10},{10,12},{12... | collective-permute-start | bytes 786440 | tf_op jit(solution)/shard_map/ppermute | solution.py:333
  27.1 13.7 %collective-permute-start.5 = (bf16[256,512]{1,0:T(8,128)(2,1)S(1)}, bf16[256,512]{1,0:T(8,128)(2,1)S(1)}, u32[]{:S(2)}, u32[]{:S(2)}) collective-permute-start(bf16[256,512]{1,0:T(8,128)(2,1)S(1)} %get-tuple-element.69), channel_id=1, source_target_pairs={{0,4},{2,6},{4,0},{6,2},{1,5},{3,7},{5,1},{7,3},{8,12},{10,14},{12... | collective-permute-start | bytes 786440 | tf_op jit(solution)/shard_map/ppermute | solution.py:333
  29.7 11.1 %collective-permute-start.6 = (bf16[256,512]{1,0:T(8,128)(2,1)S(1)}, bf16[256,512]{1,0:T(8,128)(2,1)S(1)}, u32[]{:S(2)}, u32[]{:S(2)}) collective-permute-start(bf16[256,512]{1,0:T(8,128)(2,1)S(1)} %get-tuple-element.69), channel_id=1, source_target_pairs={{0,6},{2,0},{4,2},{6,4},{1,7},{3,1},{5,3},{7,5},{8,14},{10,8},{12,... | collective-permute-start | bytes 786440 | tf_op jit(solution)/shard_map/ppermute | solution.py:333
  40.9 2.2 copy-start.14
  40.9 16.3 %copy-start.10 = (s32[1,224]{1,0:T(1,128)S(1)}, s32[1,224]{1,0:T(1,128)}, u32[]{:S(2)}) copy-start(s32[1,224]{1,0:T(1,128)} %param.16) | copy-start | bytes 2692
  40.9 16.3 %copy-start.11 = (s32[1,224]{1,0:T(1,128)S(1)}, s32[1,224]{1,0:T(1,128)}, u32[]{:S(2)}) copy-start(s32[1,224]{1,0:T(1,128)} %param.17) | copy-start | bytes 2692
  40.9 16.3 %copy-start.12 = (s32[1,224]{1,0:T(1,128)S(1)}, s32[1,224]{1,0:T(1,128)}, u32[]{:S(2)}) copy-start(s32[1,224]{1,0:T(1,128)} %param.19) | copy-start | bytes 2692
  40.9 16.3 %copy-start.13 = (s32[1,224]{1,0:T(1,128)S(1)}, s32[1,224]{1,0:T(1,128)}, u32[]{:S(2)}) copy-start(s32[1,224]{1,0:T(1,128)} %param.20) | copy-start | bytes 2692
  41.2 22.8 %collective-permute-start.7 = (bf16[4,256,512]{2,1,0:T(8,128)(2,1)S(1)}, bf16[4,256,512]{2,1,0:T(8,128)(2,1)S(1)}, u32[]{:S(2)}, u32[]{:S(2)}) collective-permute-start(bf16[4,256,512]{2,1,0:T(8,128)(2,1)S(1)} %pad_maximum_fusion.1), channel_id=1, source_target_pairs={{0,1},{1,0},{2,3},{3,2},{4,5},{5,4},{6,7},{7,6},{8,9},{9,8},{10,11... | collective-permute-start | bytes 3145736 | tf_op jit(solution)/shard_map/ppermute | solution.py:315
  43.1 9.5 %collective-permute-start = (bf16[7,128,128]{2,1,0:T(8,128)(2,1)S(1)}, bf16[7,128,128]{2,1,0:T(8,128)(2,1)S(1)}, u32[]{:S(2)}, u32[]{:S(2)}) collective-permute-start(bf16[7,128,128]{2,1,0:T(8,128)(2,1)S(1)} %bitcast.52), channel_id=1, source_target_pairs={{0,0},{128,1},{136,8},{8,9},{16,16},{144,17},{152,24},{24,25},{32,... | collective-permute-start | bytes 688136 | tf_op jit(solution)/shard_map/ppermute | solution.py:309
  45.0 19.0 %collective-permute-start.8 = (bf16[128,1792]{1,0:T(8,128)(2,1)}, bf16[128,1792]{1,0:T(8,128)(2,1)}, u32[]{:S(2)}, u32[]{:S(2)}) collective-permute-start(bf16[128,1792]{1,0:T(8,128)(2,1)} %param.13), channel_id=1, source_target_pairs={{0,0},{128,1},{136,8},{8,9},{16,16},{144,17},{152,24},{24,25},{32,... | collective-permute-start | bytes 1376264 | tf_op jit(solution)/shard_map/ppermute | solution.py:309
  52.6 9.6 %collective-permute-start.1 = (bf16[7,128,128]{2,1,0:T(8,128)(2,1)S(1)}, bf16[7,128,128]{2,1,0:T(8,128)(2,1)}, u32[]{:S(2)}, u32[]{:S(2)}) collective-permute-start(bf16[7,128,128]{2,1,0:T(8,128)(2,1)S(1)} %collective-permute-done), channel_id=1, source_target_pairs={{0,64},{64,0},{1,65},{65,1},{2,66},{66,2},{3,67},{67,3},{4,68},{68... | collective-permute-start | bytes 688136 | tf_op jit(solution)/shard_map/ppermute | solution.py:318
  57.3 1.2 collective-permute-start.9
  64.0 131.3 %reduce-scatter.5.cloned.1.call-start = ((), (), s32[]{:S(2)}) async-start(), calls=%async_computation.5 | async-start | bytes 4128768 | tf_op jit(solution)/shard_map/reduce_scatter | solution.py:380
  64.1 40.6 %collective-permute-start.12 = (bf16[56,128,128]{2,1,0:T(8,128)(2,1)}, bf16[56,128,128]{2,1,0:T(8,128)(2,1)}, u32[]{:S(2)}, u32[]{:S(2)}) collective-permute-start(bf16[56,128,128]{2,1,0:T(8,128)(2,1)} %all-gather.3.cloned.1.call-done.refs_0_), channel_id=1, source_target_pairs={{0,64},{64,0},{1,65},{65,1},{2,66},{66,2},{3,67},{67,3},{4,68},{68... | collective-permute-start | bytes 5505032 | tf_op jit(solution)/shard_map/ppermute | solution.py:318
  69.7 3.0 %copy-start = (bf16[256,4,2,512]{0,3,2,1:T(8,128)(2,1)}, bf16[256,4,2,512]{0,3,2,1:T(8,128)(2,1)S(1)}, u32[]{:S(2)}) copy-start(bf16[256,4,2,512]{0,3,2,1:T(8,128)(2,1)S(1)} %copy.19) | copy-start | bytes 6291460
  110.8 13.7 %copy-start.6 = (f32[128,1792]{1,0:T(8,128)S(1)}, f32[128,1792]{1,0:T(8,128)}, u32[]{:S(2)}) copy-start(f32[128,1792]{1,0:T(8,128)} %get-tuple-element.37) | copy-start | bytes 2752516
  110.8 11.4 %collective-permute-start.13 = (f32[128,1792]{1,0:T(8,128)}, f32[128,1792]{1,0:T(8,128)S(1)}, u32[]{:S(2)}, u32[]{:S(2)}) collective-permute-start(f32[128,1792]{1,0:T(8,128)} %get-tuple-element.38), channel_id=1, source_target_pairs={{0,1},{1,0},{2,3},{3,2},{4,5},{5,4},{6,7},{7,6},{8,9},{9,8},{10,11... | collective-permute-start | bytes 2752520 | tf_op jit(solution)/shard_map/ppermute | solution.py:315
  121.4 3.1 %collective-permute-start.10 = (f32[128,1792]{1,0:T(8,128)}, f32[128,1792]{1,0:T(8,128)S(1)}, u32[]{:S(2)}, u32[]{:S(2)}) collective-permute-start(f32[128,1792]{1,0:T(8,128)} %get-tuple-element.35), channel_id=1, source_target_pairs={{0,1},{1,0},{2,3},{3,2},{4,5},{5,4},{6,7},{7,6},{8,9},{9,8},{10,11... | collective-permute-start | bytes 2752520 | tf_op jit(solution)/shard_map/ppermute | solution.py:315
  127.2 1.8 copy-start.1
  127.2 8.8 %copy-start.2 = (bf16[128,1792]{1,0:T(8,128)(2,1)}, bf16[128,1792]{1,0:T(8,128)(2,1)S(1)}, u32[]{:S(2)}) copy-start(bf16[128,1792]{1,0:T(8,128)(2,1)S(1)} %get-tuple-element.58.own_g_ref) | copy-start | bytes 1376260
  127.2 1.8 collective-permute-start.14
  129.0 0.8 copy-start.3
  135.9 94.5 %reduce-scatter.3.cloned.1.call-start = ((), (), s32[]{:S(2)}) async-start(), calls=%async_computation.4 | async-start | bytes 2064384 | tf_op jit(solution)/shard_map/reduce_scatter | solution.py:401
  136.0 2.1 collective-permute-start.11
  138.1 0.8 copy-start.7
  144.7 41.5 %collective-permute-start.15 = (bf16[56,128,128]{2,1,0:T(8,128)(2,1)}, bf16[56,128,128]{2,1,0:T(8,128)(2,1)S(1)}, u32[]{:S(2)}, u32[]{:S(2)}) collective-permute-start(bf16[56,128,128]{2,1,0:T(8,128)(2,1)} %get-tuple-element.43), channel_id=1, source_target_pairs={{0,64},{64,0},{1,65},{65,1},{2,66},{66,2},{3,67},{67,3},{4,68},{68... | collective-permute-start | bytes 5505032 | tf_op jit(solution)/shard_map/ppermute | solution.py:318
  160.0 3.3 %collective-permute-start.16 = (bf16[2,4,128,512]{3,2,1,0:T(8,128)(2,1)}, bf16[2,4,128,512]{3,2,1,0:T(8,128)(2,1)S(1)}, u32[]{:S(2)}, u32[]{:S(2)}) collective-permute-start(bf16[2,4,128,512]{3,2,1,0:T(8,128)(2,1)} %get-tuple-element.48), channel_id=1, source_target_pairs={{0,1},{1,0},{2,3},{3,2},{4,5},{5,4},{6,7},{7,6},{8,9},{9,8},{10,11... | collective-permute-start | bytes 3145736 | tf_op jit(solution)/shard_map/ppermute | solution.py:315
  163.3 1.0 copy-start.5
  164.3 22.0 %copy-start.4 = (bf16[56,128,128]{2,1,0:T(8,128)(2,1)S(1)}, bf16[56,128,128]{2,1,0:T(8,128)(2,1)}, u32[]{:S(2)}) copy-start(bf16[56,128,128]{2,1,0:T(8,128)(2,1)} %get-tuple-element.42) | copy-start | bytes 5505028
  188.2 15.3 %collective-permute-start.17 = (bf16[4,128,512]{2,1,0:T(8,128)(2,1)S(1)}, bf16[4,128,512]{2,1,0:T(8,128)(2,1)S(1)}, u32[]{:S(2)}, u32[]{:S(2)}) collective-permute-start(bf16[4,128,512]{2,1,0:T(8,128)(2,1)S(1)} %dynamic-slice_bitcast_fusion), channel_id=1, source_target_pairs={{0,128},{128,0},{1,129},{129,1},{2,130},{130,2},{3,131},{131,3},{4... | collective-permute-start | bytes 1572872 | tf_op jit(solution)/shard_map/ppermute | solution.py:402
  192.4 33.5 %collective-permute-start.22 = (bf16[128,1792]{1,0:T(8,128)(2,1)}, bf16[128,1792]{1,0:T(8,128)(2,1)S(1)}, u32[]{:S(2)}, u32[]{:S(2)}) collective-permute-start(bf16[128,1792]{1,0:T(8,128)(2,1)} %get-tuple-element.51), channel_id=1, source_target_pairs={{0,0},{1,128},{8,136},{9,8},{16,16},{17,144},{24,152},{25,24},{32,... | collective-permute-start | bytes 1376264 | tf_op jit(solution)/shard_map/ppermute | solution.py:312
  195.3 19.3 %copy-start.8 = (bf16[14,128,128]{2,1,0:T(8,128)(2,1)S(1)}, bf16[14,128,128]{2,1,0:T(8,128)(2,1)}, u32[]{:S(2)}) copy-start(bf16[14,128,128]{2,1,0:T(8,128)(2,1)} %reduce-scatter.5.cloned.1.call-done) | copy-start | bytes 1376260
  196.4 18.3 %collective-permute-start.23 = (bf16[7,128,128]{2,1,0:T(8,128)(2,1)S(1)}, bf16[7,128,128]{2,1,0:T(8,128)(2,1)S(1)}, u32[]{:S(2)}, u32[]{:S(2)}) collective-permute-start(bf16[7,128,128]{2,1,0:T(8,128)(2,1)S(1)} %slice.9), channel_id=1, source_target_pairs={{0,64},{64,0},{1,65},{65,1},{2,66},{66,2},{3,67},{67,3},{4,68},{68... | collective-permute-start | bytes 688136 | tf_op jit(solution)/shard_map/ppermute | solution.py:318
  203.7 18.4 %collective-permute-start.18 = (bf16[128,512]{1,0:T(8,128)(2,1)S(1)}, bf16[128,512]{1,0:T(8,128)(2,1)S(1)}, u32[]{:S(2)}, u32[]{:S(2)}) collective-permute-start(bf16[128,512]{1,0:T(8,128)(2,1)S(1)} %get-tuple-element.65), channel_id=1, source_target_pairs={{0,2},{2,4},{4,6},{6,0},{1,3},{3,5},{5,7},{7,1},{8,10},{10,12},{12... | collective-permute-start | bytes 393224 | tf_op jit(solution)/shard_map/ppermute | solution.py:406
  210.1 12.0 %collective-permute-start.19 = (bf16[128,512]{1,0:T(8,128)(2,1)S(1)}, bf16[128,512]{1,0:T(8,128)(2,1)S(1)}, u32[]{:S(2)}, u32[]{:S(2)}) collective-permute-start(bf16[128,512]{1,0:T(8,128)(2,1)S(1)} %get-tuple-element.67), channel_id=1, source_target_pairs={{0,4},{2,6},{4,0},{6,2},{1,5},{3,7},{5,1},{7,3},{8,12},{10,14},{12... | collective-permute-start | bytes 393224 | tf_op jit(solution)/shard_map/ppermute | solution.py:406
  210.1 12.0 %collective-permute-start.20 = (bf16[128,512]{1,0:T(8,128)(2,1)S(1)}, bf16[128,512]{1,0:T(8,128)(2,1)S(1)}, u32[]{:S(2)}, u32[]{:S(2)}) collective-permute-start(bf16[128,512]{1,0:T(8,128)(2,1)S(1)} %get-tuple-element.66), channel_id=1, source_target_pairs={{0,6},{2,0},{4,2},{6,4},{1,7},{3,1},{5,3},{7,5},{8,14},{10,8},{12,... | collective-permute-start | bytes 393224 | tf_op jit(solution)/shard_map/ppermute | solution.py:406
  214.7 15.7 %collective-permute-start.24 = (bf16[7,128,128]{2,1,0:T(8,128)(2,1)S(1)}, bf16[7,128,128]{2,1,0:T(8,128)(2,1)S(1)}, u32[]{:S(2)}, u32[]{:S(2)}) collective-permute-start(bf16[7,128,128]{2,1,0:T(8,128)(2,1)S(1)} %multiply_convert_fusion.2), channel_id=1, source_target_pairs={{0,0},{1,128},{8,136},{9,8},{16,16},{17,144},{24,152},{25,24},{32,... | collective-permute-start | bytes 688136 | tf_op jit(solution)/shard_map/ppermute | solution.py:312
  222.3 7.8 %collective-permute-start.21 = (bf16[128,512]{1,0:T(8,128)(2,1)S(1)}, bf16[128,512]{1,0:T(8,128)(2,1)S(1)}, u32[]{:S(2)}, u32[]{:S(2)}) collective-permute-start(bf16[128,512]{1,0:T(8,128)(2,1)S(1)} %fusion.7), channel_id=1, source_target_pairs={{0,0},{1,128},{8,136},{9,8},{16,16},{17,144},{24,152},{25,24},{32,... | collective-permute-start | bytes 393224 | tf_op jit(solution)/shard_map/ppermute | solution.py:312
  231.4 12.8 %collective-permute-start.25 = (bf16[7,128,128]{2,1,0:T(8,128)(2,1)S(1)}, bf16[7,128,128]{2,1,0:T(8,128)(2,1)S(1)}, u32[]{:S(2)}, u32[]{:S(2)}) collective-permute-start(bf16[7,128,128]{2,1,0:T(8,128)(2,1)S(1)} %multiply_convert_fusion.1), channel_id=1, source_target_pairs={{0,0},{1,128},{8,136},{9,8},{16,16},{17,144},{24,152},{25,24},{32,... | collective-permute-start | bytes 688136 | tf_op jit(solution)/shard_map/ppermute | solution.py:312
Sparse Core Ops, SparseCore 0:
  18.0 39.8 all-gather.2
  64.1 50.8 all-gather.4
  136.1 54.0 reduce-scatter.4
  192.6 37.7 reduce-scatter.2
